TPU v7x, 32 devices: a whole 2x2x4 slice. The times are simulated.
32 devices in a mesh: dp: 8 (over z, core), row: 2 (over x), col: 2 (over y).
Axes of the slice: x: 2, y: 2, z: 4, core: 2. Of those that a mesh axis runs over, the one named last changes fastest.
Arguments:
- tokens: bfloat16 [2, 16384, 768], P(None, ('dp', 'col'), 'row'), may hold values from -6 to 6
- joint_weight: bfloat16 [768, 3, 768], P('row', None, 'col'), may hold values from -0.3125 to 0.3125
- joint_bias: float32 [2, 768], P(None, 'col'), may hold values from -1.75 to 1.75
- out_weight: bfloat16 [768, 768], P('col', 'row'), may hold values from -1.75 to 1.75
- out_bias: float32 [768], P('row'), may hold values from -1.75 to 1.75
- norm_gain: float32 [768], P('row'), may hold values from 0.5 to 1.5
- norm_shift: float32 [768], P('row'), may hold values from -1.75 to 1.75
- inner_weight: bfloat16 [768, 3072], P('row', 'col'), may hold values from -0.21875 to 0.21875
- inner_bias: float32 [3072], P('col'), may hold values from -1.75 to 1.75
- outer_weight: bfloat16 [3072, 768], P('col', 'row'), may hold values from -0.21875 to 0.21875
- outer_bias: float32 [768], P('row'), may hold values from -1.75 to 1.75
- final_gain: float32 [768], P('row'), may hold values from 0.5 to 1.5
- final_shift: float32 [768], P('row'), may hold values from -1.75 to 1.75
- trained_gate_scores: float32 [12, 512, 512], P('col'), may hold values from -6 to 6
- mask_noise: float32 [12, 512, 512], P('col'), may hold values from 0.02 to 0.98
- cotangent: bfloat16 [2, 16384, 768], P(None, ('dp', 'col'), 'row'), may hold values from -6 to 6
Outputs:
- output: bfloat16 [2, 16384, 768], P(None, ('dp', 'col'), 'row')
- grad_tokens: float32 [2, 16384, 768], P(None, ('dp', 'col'), 'row')
- grad_joint_weight: float32 [768, 3, 768], P('row', None, 'col')
- grad_joint_bias: float32 [2, 768], P(None, 'col')
- grad_out_weight: float32 [768, 768], P('col', 'row')
- grad_out_bias: float32 [768], P('row')
- grad_norm_gain: float32 [768], P('row')
- grad_norm_shift: float32 [768], P('row')
- grad_inner_weight: float32 [768, 3072], P('row', 'col')
- grad_inner_bias: float32 [3072], P('col')
- grad_outer_weight: float32 [3072, 768], P('col', 'row')
- grad_outer_bias: float32 [768], P('row')
- grad_final_gain: float32 [768], P('row')
- grad_final_shift: float32 [768], P('row')
- grad_mask_logit: float32 [12, 512, 512], P('col', ('dp', 'row'))
All inputs are finite; a program needn't handle non-finite values.
Results may differ from a plain program's by a relative error of at most 0.02.
Values may be sent and summed in bfloat16 or wider, within the bound.
No kernel may reach another device: no remote copies, remote signals or barrier semaphores. Data moves between devices by JAX's collectives and lax.ppermute only.
A program may use at most 896 MiB of HBM per device.

v0:
```python
import jax
import jax.numpy as jnp
from jax import lax
from jax.sharding import PartitionSpec as P

D = 768
HDIM = 64
MASK_LEN = 512
PROMPT = 1024
CONT_LEN = 512


relaxation_heat = 0.75
norm_eps = 1e-12
masked_score = -1e30


def gather_cols(local):
    return lax.all_gather(local, "col", axis=0, tiled=True)


def gather_rows(local):
    return lax.all_gather(local, "row", axis=0, tiled=True)


def multiply(block, weight, flipped):
    if flipped:
        return lax.dot_general(
            block, weight, (((1,), (1,)), ((), ())), preferred_element_type=jnp.float32
        )
    return jnp.dot(block, weight, preferred_element_type=jnp.float32)


def sum_over_rows(whole, weight, flipped):

    def partial_rows(first, number):
        return multiply(whole, weight, flipped)

    return lax.psum_scatter(
        partial_rows(jnp.int32(0), whole.shape[0] // lax.axis_size("row") * lax.axis_size("row")),
        "row",
        scatter_dimension=0,
        tiled=True,
    )


def sum_over_cols(whole, weight, flipped):

    def partial_rows(first, number):
        return multiply(whole, weight, flipped)

    return lax.psum_scatter(
        partial_rows(jnp.int32(0), whole.shape[0] // lax.axis_size("col") * lax.axis_size("col")),
        "col",
        scatter_dimension=0,
        tiled=True,
    )


def transpose_product(left, right):
    return lax.dot_general(
        left, right, (((0,), (0,)), ((), ())), preferred_element_type=jnp.float32
    )


def row_totals(first, second):
    return lax.psum((jnp.sum(first, axis=-1), jnp.sum(second, axis=-1)), "row")


def norm_forward(values, gain, shift):
    total, squares = row_totals(values, values * values)
    mean = total / D
    spread = squares / D - mean * mean
    scale = lax.rsqrt(spread + norm_eps)[:, None]
    normed = (values - mean[:, None]) * scale
    return (normed, scale, normed * gain + shift)


def norm_backward(grad_out, normed, scale, gain):
    scaled = grad_out * gain
    total, mixed = row_totals(scaled, scaled * normed)
    return scale * (scaled - total[:, None] / D - normed * mixed[:, None] / D)


def exact_gelu(values):
    return jax.nn.gelu(values, approximate=False)


def window_rows(whole, window_start, window, heads_here):
    joined = jnp.concatenate(
        [whole[:PROMPT], lax.dynamic_slice_in_dim(whole, window_start, window, 0)], 0
    )
    return joined.reshape(PROMPT + window, heads_here, HDIM)


def spread_rows(grad_cat, window_start, group_rows):
    width = grad_cat.shape[1] * grad_cat.shape[2]
    flat = grad_cat.reshape(grad_cat.shape[0], width)
    full = jnp.concatenate([flat[:PROMPT], jnp.zeros((group_rows - PROMPT, width), jnp.float32)], 0)
    window_part = flat[PROMPT:]
    current = lax.dynamic_slice_in_dim(full, window_start, window_part.shape[0], 0)
    return lax.dynamic_update_slice_in_dim(full, current + window_part, window_start, 0)


def score_table(query, keys_cat, visible):
    scores = jnp.einsum(
        "qhd,khd->hqk", query, keys_cat, preferred_element_type=jnp.float32
    ) * HDIM ** (-0.5)
    return jnp.where(visible[None], scores, masked_score)


def attend(query, keys_cat, values_cat, visible, mask_table):
    scores = score_table(query, keys_cat, visible)
    peak = jnp.max(scores, axis=-1, keepdims=True)
    expo = jnp.exp(scores - peak)
    total = jnp.sum(expo, axis=-1, keepdims=True)
    weights = (expo / total * mask_table).astype(jnp.bfloat16)
    mixed = jnp.einsum("hqk,khd->qhd", weights, values_cat, preferred_element_type=jnp.float32)
    return (mixed, peak + jnp.log(total))


def attend_back(query, keys_cat, values_cat, visible, mask_table, log_total, grad_mixed):
    prob = jnp.exp(score_table(query, keys_cat, visible) - log_total)
    weights = (prob * mask_table).astype(jnp.bfloat16)
    value_sensitivity = jnp.einsum(
        "hqk,qhd->khd", weights, grad_mixed, preferred_element_type=jnp.float32
    )
    grad_weights = jnp.einsum(
        "qhd,khd->hqk", grad_mixed, values_cat, preferred_element_type=jnp.float32
    )
    grad_prob = grad_weights * mask_table
    grad_scores = prob * (grad_prob - jnp.sum(grad_prob * prob, axis=-1, keepdims=True))
    grad_low = grad_scores.astype(jnp.bfloat16)
    grad_query = jnp.einsum(
        "hqk,khd->qhd", grad_low, keys_cat, preferred_element_type=jnp.float32
    ) * HDIM ** (-0.5)
    grad_keys = jnp.einsum(
        "hqk,qhd->khd", grad_low, query, preferred_element_type=jnp.float32
    ) * HDIM ** (-0.5)
    return (grad_query, grad_keys, value_sensitivity, grad_weights * prob)


def fold_mask(part, row_offset):
    heads_here, block_rows, width = part.shape
    folded = part.reshape(heads_here, block_rows, width // MASK_LEN, MASK_LEN).sum(2)
    if block_rows >= MASK_LEN:
        return folded.reshape(heads_here, block_rows // MASK_LEN, MASK_LEN, MASK_LEN).sum(1)
    blank = jnp.zeros((heads_here, MASK_LEN, MASK_LEN), jnp.float32)
    return lax.dynamic_update_slice_in_dim(blank, folded, row_offset, 1)


def reduce_params(weight_part, norm_part):
    weight_sum = (
        lax.psum(weight_part[0].astype(jnp.bfloat16), "dp").astype(jnp.float32),
        lax.psum(weight_part[1].astype(jnp.bfloat16), "dp").astype(jnp.float32),
        lax.psum(weight_part[2].astype(jnp.bfloat16), "dp").astype(jnp.float32),
        lax.psum(weight_part[3].astype(jnp.bfloat16), "dp").astype(jnp.float32),
        lax.psum(weight_part[4].astype(jnp.bfloat16), "dp").astype(jnp.float32),
        lax.psum(weight_part[5].astype(jnp.bfloat16), "dp").astype(jnp.float32),
        lax.psum(weight_part[6].astype(jnp.bfloat16), "dp").astype(jnp.float32),
        lax.psum(weight_part[7].astype(jnp.bfloat16), "dp").astype(jnp.float32),
    )
    norm_sum = lax.psum((norm_part[0], norm_part[1], norm_part[2], norm_part[3]), ("dp", "col"))
    return (tuple(weight_sum), tuple(norm_sum))


def collapse_mask_gradient(mask_part):
    return lax.psum_scatter(mask_part, ("dp", "row"), scatter_dimension=1, tiled=True)


def on_device(
    tokens,
    joint_weight,
    joint_bias,
    out_weight,
    out_bias,
    norm_gain,
    norm_shift,
    inner_weight,
    inner_bias,
    outer_weight,
    outer_bias,
    final_gain,
    final_shift,
    trained_gate_scores,
    mask_noise,
    cotangent,
):
    micro, half_rows, row_width = tokens.shape
    heads_here = trained_gate_scores.shape[0]
    col_width = joint_weight.shape[2]
    joint_flat = joint_weight.reshape(row_width, 3 * col_width)
    sigmoid_squash = jnp.log(mask_noise) - jnp.log1p(-mask_noise)
    gate_open_chance = jax.nn.sigmoid((trained_gate_scores + sigmoid_squash) / relaxation_heat)
    group_rows = half_rows * lax.axis_size("col")
    block_rows = group_rows // lax.axis_size("row")
    window = max(block_rows, CONT_LEN)
    start = lax.axis_index("row") * block_rows
    window_start = start - start % window
    row_offset = start % MASK_LEN
    query_pos = start + jnp.arange(block_rows, dtype=jnp.int32)
    key_pos = window_start + jnp.arange(window, dtype=jnp.int32)
    same = (query_pos[:, None] - PROMPT) // CONT_LEN == (key_pos[None, :] - PROMPT) // CONT_LEN
    tail = (query_pos[:, None] >= PROMPT) & (key_pos[None, :] >= PROMPT) & same
    visible = jnp.concatenate([jnp.ones((block_rows, PROMPT), jnp.bool_), tail], 1)
    if block_rows >= MASK_LEN:
        mask_rows = jnp.tile(gate_open_chance, (1, block_rows // MASK_LEN, 1))
    else:
        mask_rows = lax.dynamic_slice_in_dim(gate_open_chance, row_offset, block_rows, 1)
    mask_table = jnp.tile(mask_rows, (1, 1, (PROMPT + window) // MASK_LEN))
    bias_rows = jnp.stack([joint_bias[0], jnp.zeros_like(joint_bias[0]), joint_bias[1]])
    weight_acc = (
        jnp.zeros((row_width, 3 * col_width), jnp.float32),
        jnp.zeros((2, col_width), jnp.float32),
        jnp.zeros(out_weight.shape, jnp.float32),
        jnp.zeros(out_bias.shape, jnp.float32),
        jnp.zeros(inner_weight.shape, jnp.float32),
        jnp.zeros(inner_bias.shape, jnp.float32),
        jnp.zeros(outer_weight.shape, jnp.float32),
        jnp.zeros(outer_bias.shape, jnp.float32),
    )
    norm_acc = (
        jnp.zeros((row_width,), jnp.float32),
        jnp.zeros((row_width,), jnp.float32),
        jnp.zeros((row_width,), jnp.float32),
        jnp.zeros((row_width,), jnp.float32),
    )
    gate_running_total = jnp.zeros(gate_open_chance.shape, jnp.float32)
    outcome_list = []
    grad_list = []
    for micro_index in range(micro):
        source = tokens[micro_index]
        source_all = gather_cols(source)
        joint_raw = (
            sum_over_rows(source_all, joint_flat, False).reshape(block_rows, 3, col_width)
            + bias_rows
        )
        joint_low = joint_raw.astype(jnp.bfloat16)
        keys_all, values_all = (
            lax.all_gather(joint_low[:, 1], "row", axis=0, tiled=True),
            lax.all_gather(joint_low[:, 2], "row", axis=0, tiled=True),
        )
        keys_cat = window_rows(keys_all, window_start, window, heads_here)
        values_cat = window_rows(values_all, window_start, window, heads_here)
        query = joint_low[:, 0].reshape(block_rows, heads_here, HDIM)
        mixed, log_total = attend(query, keys_cat, values_cat, visible, mask_table)
        attended_all = gather_rows(mixed.reshape(block_rows, col_width).astype(jnp.bfloat16))
        branch = sum_over_cols(attended_all, out_weight, False) + out_bias
        normed_one, scale_one, hidden = norm_forward(
            source.astype(jnp.float32) + branch, norm_gain, norm_shift
        )
        hidden_all = gather_cols(hidden.astype(jnp.bfloat16))
        inner = sum_over_rows(hidden_all, inner_weight, False) + inner_bias
        active, gelu_pull = jax.vjp(exact_gelu, inner)
        active_all = gather_rows(active.astype(jnp.bfloat16))
        outer = sum_over_cols(active_all, outer_weight, False) + outer_bias
        normed_two, scale_two, result = norm_forward(hidden + outer, final_gain, final_shift)
        outcome_list.append(result.astype(jnp.bfloat16))
        grad_result = cotangent[micro_index].astype(jnp.float32)
        final_gain_part = jnp.sum(grad_result * normed_two, axis=0)
        final_shift_part = jnp.sum(grad_result, axis=0)
        grad_second = norm_backward(grad_result, normed_two, scale_two, final_gain)
        grad_outer_all = gather_cols(grad_second.astype(jnp.bfloat16))
        outer_weight_part = transpose_product(active_all, grad_outer_all)
        outer_bias_part = jnp.sum(grad_outer_all.astype(jnp.float32), axis=0)
        grad_active = sum_over_rows(grad_outer_all, outer_weight, True)
        grad_inner_all = gather_rows(gelu_pull(grad_active)[0].astype(jnp.bfloat16))
        inner_weight_part = transpose_product(hidden_all, grad_inner_all)
        inner_bias_part = jnp.sum(grad_inner_all.astype(jnp.float32), axis=0)
        grad_hidden = sum_over_cols(grad_inner_all, inner_weight, True) + grad_second
        norm_gain_part = jnp.sum(grad_hidden * normed_one, axis=0)
        norm_shift_part = jnp.sum(grad_hidden, axis=0)
        grad_first = norm_backward(grad_hidden, normed_one, scale_one, norm_gain)
        grad_branch_all = gather_cols(grad_first.astype(jnp.bfloat16))
        out_weight_part = transpose_product(attended_all, grad_branch_all)
        out_bias_part = jnp.sum(grad_branch_all.astype(jnp.float32), axis=0)
        grad_attended = sum_over_rows(grad_branch_all, out_weight, True)
        grad_mixed = grad_attended.astype(jnp.bfloat16).reshape(block_rows, heads_here, HDIM)
        grad_query, grad_keys_cat, grad_values_cat, mask_part = attend_back(
            query, keys_cat, values_cat, visible, mask_table, log_total, grad_mixed
        )
        gate_running_total = gate_running_total + fold_mask(mask_part, row_offset)
        key_full = spread_rows(grad_keys_cat, window_start, group_rows)
        value_full = spread_rows(grad_values_cat, window_start, group_rows)
        grad_keys, value_sensitivity = (
            lax.psum_scatter(
                key_full.astype(jnp.bfloat16), "row", scatter_dimension=0, tiled=True
            ).astype(jnp.float32),
            lax.psum_scatter(
                value_full.astype(jnp.bfloat16), "row", scatter_dimension=0, tiled=True
            ).astype(jnp.float32),
        )
        grad_joint = jnp.stack(
            [grad_query.reshape(block_rows, col_width), grad_keys, value_sensitivity], 1
        )
        grad_joint_all = gather_rows(
            grad_joint.astype(jnp.bfloat16).reshape(block_rows, 3 * col_width)
        )
        joint_weight_part = transpose_product(source_all, grad_joint_all)
        joint_sums = jnp.sum(grad_joint_all.astype(jnp.float32), axis=0).reshape(3, col_width)
        joint_bias_part = jnp.stack([joint_sums[0], joint_sums[2]])
        grad_list.append(sum_over_cols(grad_joint_all, joint_flat, True) + grad_first)
        weight_step = (
            joint_weight_part,
            joint_bias_part,
            out_weight_part,
            out_bias_part,
            inner_weight_part,
            inner_bias_part,
            outer_weight_part,
            outer_bias_part,
        )
        norm_step = (norm_gain_part, norm_shift_part, final_gain_part, final_shift_part)
        weight_acc = jax.tree.map(jnp.add, weight_acc, weight_step)
        norm_acc = jax.tree.map(jnp.add, norm_acc, norm_step)
    weight_acc, norm_acc = reduce_params(weight_acc, norm_acc)
    gate_backward_factor = collapse_mask_gradient(
        gate_running_total * gate_open_chance * (1.0 - gate_open_chance) / relaxation_heat
    )
    return (
        jnp.stack(outcome_list),
        jnp.stack(grad_list),
        weight_acc[0].reshape(row_width, 3, col_width),
        weight_acc[1],
        weight_acc[2],
        weight_acc[3],
        norm_acc[0],
        norm_acc[1],
        weight_acc[4],
        weight_acc[5],
        weight_acc[6],
        weight_acc[7],
        norm_acc[2],
        norm_acc[3],
        gate_backward_factor,
    )


def solution(mesh):
    placed = (
        P(None, ("dp", "col"), "row"),
        P("row", None, "col"),
        P(None, "col"),
        P("col", "row"),
        P("row"),
        P("row"),
        P("row"),
        P("row", "col"),
        P("col"),
        P("col", "row"),
        P("row"),
        P("row"),
        P("row"),
        P("col", None, None),
        P("col", None, None),
        P(None, ("dp", "col"), "row"),
    )
    return jax.shard_map(
        on_device,
        mesh=mesh,
        in_specs=placed,
        out_specs=(
            P(None, ("dp", "col"), "row"),
            P(None, ("dp", "col"), "row"),
            P("row", None, "col"),
            P(None, "col"),
            P("col", "row"),
            P("row"),
            P("row"),
            P("row"),
            P("row", "col"),
            P("col"),
            P("col", "row"),
            P("row"),
            P("row"),
            P("row"),
            P("col", ("dp", "row"), None),
        ),
        check_vma=False,
    )
```

profile of v0, /device:TPU:0, one launch (start us, length us, event | category | flops | bytes accessed | tf_op | source)
XLA Modules:
  0.0 3165.0 jit_solution(13070523617022897723)
XLA Ops:
  13.3 26.9 all-gather.61.cloned.1.call-done
  48.1 21.4 all-gather.55.cloned.1.call-done
  78.1 104.4 %reduce-scatter.30.cloned.1.call-done = f32[1024,1152]{1,0:T(8,128)} async-done(((f32[2048,1152]{1,0:T(8,128)}), f32[1024,1152]{1,0:T(8,128)}) %reduce-scatter.30.cloned.1.call-update) | async-done | bytes 4718608 | tf_op jit(solution)/shard_map/reduce_scatter | solution.py:39
  188.5 106.7 %reduce-scatter.22.cloned.1.call-done = f32[1024,1152]{1,0:T(8,128)} async-done(((f32[2048,1152]{1,0:T(8,128)}), f32[1024,1152]{1,0:T(8,128)}) %reduce-scatter.22.cloned.1.call-update) | async-done | bytes 4718608 | tf_op jit(solution)/shard_map/reduce_scatter | solution.py:39
  343.2 59.3 %tile.19 = f32[6,1024,2048]{2,1,0:T(8,128)} reshape(f32[6,1024,4,512]{3,2,1,0:T(4,128)} %tile.18) | data formatting | bytes 100663296 | tf_op jit(solution)/shard_map/tile | solution.py:210
  427.9 22.1 fusion.2
  449.9 22.6 fusion
  472.6 34.4 %fusion.53 = bf16[6,64,1024]{2,1,0:T(8,128)(2,1)} fusion(bf16[2048,6,64]{0,2,1:T(8,128)(2,1)} %bitcast.237, f32[6,1024,2048]{2,1,0:T(8,128)} %tile.19, f32[6,1024,2048]{2,1,0:T(8,128)} %get-tuple-element.133, f32[6,1024]{1,0:T(8,128)S(1)} %fusion, f32[6,1024]{1,0:T(8,128)S(1)} %get-tuple-element.132, pred[1024,2048]{1,0:T(8,128)(4,1)S(1)} %concatenate.28), kind=kOutput, calls=%fused_computation.149 | convolution fusion | flops 1686503424 | bytes 105168896 | tf_op jit(solution)/shard_map/hqk,khd->qhd/dot_general | solution.py:118
  507.1 27.2 all-gather.27.cloned.1.call-done
  538.6 43.5 %reduce-scatter.24.cloned.1.call-done = f32[1024,384]{1,0:T(8,128)} async-done(((f32[2048,384]{1,0:T(8,128)}), f32[1024,384]{1,0:T(8,128)}) %reduce-scatter.24.cloned.1.call-update) | async-done | bytes 1572880 | tf_op jit(solution)/shard_map/reduce_scatter | solution.py:52
  593.0 27.1 all-gather.29.cloned.1.call-done
  629.8 144.7 %reduce-scatter.26.cloned.1.call-done = f32[1024,1536]{1,0:T(8,128)} async-done(((f32[2048,1536]{1,0:T(8,128)}), f32[1024,1536]{1,0:T(8,128)}) %reduce-scatter.26.cloned.1.call-update) | async-done | bytes 6291472 | tf_op jit(solution)/shard_map/reduce_scatter | solution.py:39
  790.6 80.5 %all-gather.31.cloned.1.call-done = bf16[2048,1536]{1,0:T(8,128)(2,1)} async-done(((bf16[1024,1536]{1,0:T(8,128)(2,1)}), bf16[2048,1536]{1,0:T(8,128)(2,1)}) %all-gather.31.cloned.1.call-update) | async-done | bytes 6291472 | tf_op jit(solution)/shard_map/all_gather | solution.py:23
  879.0 43.5 %reduce-scatter.28.cloned.1.call-done = f32[1024,384]{1,0:T(8,128)} async-done(((f32[2048,384]{1,0:T(8,128)}), f32[1024,384]{1,0:T(8,128)}) %reduce-scatter.28.cloned.1.call-update) | async-done | bytes 1572880 | tf_op jit(solution)/shard_map/reduce_scatter | solution.py:52
  942.9 27.3 all-gather.39.cloned.1.call-done
  978.5 144.3 %reduce-scatter.38.cloned.1.call-done = f32[1024,1536]{1,0:T(8,128)} async-done(((f32[2048,1536]{1,0:T(8,128)}), f32[1024,1536]{1,0:T(8,128)}) %reduce-scatter.38.cloned.1.call-update) | async-done | bytes 6291472 | tf_op jit(solution)/shard_map/reduce_scatter | solution.py:39
  1132.3 80.5 %all-gather.41.cloned.1.call-done = bf16[2048,1536]{1,0:T(8,128)(2,1)} async-done(((bf16[1024,1536]{1,0:T(8,128)(2,1)}), bf16[2048,1536]{1,0:T(8,128)(2,1)}) %all-gather.41.cloned.1.call-update) | async-done | bytes 6291472 | tf_op jit(solution)/shard_map/all_gather | solution.py:23
  1221.1 43.5 %reduce-scatter.40.cloned.1.call-done = f32[1024,384]{1,0:T(8,128)} async-done(((f32[2048,384]{1,0:T(8,128)}), f32[1024,384]{1,0:T(8,128)}) %reduce-scatter.40.cloned.1.call-update) | async-done | bytes 1572880 | tf_op jit(solution)/shard_map/reduce_scatter | solution.py:52
  1281.5 23.4 all-gather.43.cloned.1.call-done
  1309.2 24.9 all-gather.65.cloned.1.call-done
  1334.0 29.3 all-gather.63.cloned.1.call-done
  1387.3 22.2 reduce-scatter.42.cloned.1.call-done
  1414.2 20.9 fusion.115
  1435.0 95.4 %multiply_reduce_fusion.1 = (f32[6,1024]{1,0:T(8,128)}, f32[6,1024]{1,0:T(8,128)S(1)}, f32[6,1024,2048]{2,1,0:T(8,128)}, f32[6,1024,2048]{2,1,0:T(8,128)}, f32[6,1024,2048]{2,1,0:T(8,128)}) fusion(f32[6,1024]{1,0:T(8,128)S(1)} %log_add_fusion.1, f32[6,1024,2048]{2,1,0:T(8,128)} %get-tuple-element.133, pred[1024,2048]{1,0:T(8,128)(4,1)S(1)} %concatenate.28, ...), kind=kOutput, calls=%fused_computation.6 | convolution fusion | flops 1736429568 | bytes 306520064 | tf_op jit(solution)/shard_map/qhd,khd->hqk/dot_general | solution.py:106
  1530.5 22.6 fusion.1
  1553.1 34.4 %fusion.52 = bf16[6,64,1024]{2,1,0:T(8,128)(2,1)} fusion(bf16[2048,6,64]{0,2,1:T(8,128)(2,1)} %bitcast.235, f32[6,1024,2048]{2,1,0:T(8,128)} %tile.19, f32[6,1024,2048]{2,1,0:T(8,128)} %get-tuple-element.134, f32[6,1024]{1,0:T(8,128)S(1)} %fusion.1, f32[6,1024]{1,0:T(8,128)S(1)} %get-tuple-element.24, pred[1024,2048]{1,0:T(8,128)(4,1)S(1)} %concatenate.28), kind=kOutput, calls=%fused_computation.148 | convolution fusion | flops 1686503424 | bytes 105168896 | tf_op jit(solution)/shard_map/hqk,khd->qhd/dot_general | solution.py:118
  1587.8 27.1 all-gather.33.cloned.1.call-done
  1619.2 43.5 %reduce-scatter.32.cloned.1.call-done = f32[1024,384]{1,0:T(8,128)} async-done(((f32[2048,384]{1,0:T(8,128)}), f32[1024,384]{1,0:T(8,128)}) %reduce-scatter.32.cloned.1.call-update) | async-done | bytes 1572880 | tf_op jit(solution)/shard_map/reduce_scatter | solution.py:52
  1673.4 27.3 all-gather.35.cloned.1.call-done
  1710.5 144.7 %reduce-scatter.34.cloned.1.call-done = f32[1024,1536]{1,0:T(8,128)} async-done(((f32[2048,1536]{1,0:T(8,128)}), f32[1024,1536]{1,0:T(8,128)}) %reduce-scatter.34.cloned.1.call-update) | async-done | bytes 6291472 | tf_op jit(solution)/shard_map/reduce_scatter | solution.py:39
  1871.2 80.5 %all-gather.37.cloned.1.call-done = bf16[2048,1536]{1,0:T(8,128)(2,1)} async-done(((bf16[1024,1536]{1,0:T(8,128)(2,1)}), bf16[2048,1536]{1,0:T(8,128)(2,1)}) %all-gather.37.cloned.1.call-update) | async-done | bytes 6291472 | tf_op jit(solution)/shard_map/all_gather | solution.py:23
  1959.7 43.5 %reduce-scatter.36.cloned.1.call-done = f32[1024,384]{1,0:T(8,128)} async-done(((f32[2048,384]{1,0:T(8,128)}), f32[1024,384]{1,0:T(8,128)}) %reduce-scatter.36.cloned.1.call-update) | async-done | bytes 1572880 | tf_op jit(solution)/shard_map/reduce_scatter | solution.py:52
  2023.0 26.9 all-gather.47.cloned.1.call-done
  2057.9 144.7 %reduce-scatter.50.cloned.1.call-done = f32[1024,1536]{1,0:T(8,128)} async-done(((f32[2048,1536]{1,0:T(8,128)}), f32[1024,1536]{1,0:T(8,128)}) %reduce-scatter.50.cloned.1.call-update) | async-done | bytes 6291472 | tf_op jit(solution)/shard_map/reduce_scatter | solution.py:39
  2212.1 80.5 %all-gather.49.cloned.1.call-done = bf16[2048,1536]{1,0:T(8,128)(2,1)} async-done(((bf16[1024,1536]{1,0:T(8,128)(2,1)}), bf16[2048,1536]{1,0:T(8,128)(2,1)}) %all-gather.49.cloned.1.call-update) | async-done | bytes 6291472 | tf_op jit(solution)/shard_map/all_gather | solution.py:23
  2300.6 43.5 %reduce-scatter.52.cloned.1.call-done = f32[1024,384]{1,0:T(8,128)} async-done(((f32[2048,384]{1,0:T(8,128)}), f32[1024,384]{1,0:T(8,128)}) %reduce-scatter.52.cloned.1.call-update) | async-done | bytes 1572880 | tf_op jit(solution)/shard_map/reduce_scatter | solution.py:52
  2357.3 27.3 all-gather.51.cloned.1.call-done
  2389.9 34.0 %fusion.23 = f32[2048,6,64]{0,2,1:T(8,128)S(1)} fusion(bf16[1024,6,64]{0,2,1:T(8,128)(2,1)S(1)} %bitcast.207, f32[6,1024,2048]{2,1,0:T(8,128)} %tile.19, f32[6,1024]{1,0:T(8,128)S(1)} %log_add_fusion.1, f32[6,1024,2048]{2,1,0:T(8,128)} %get-tuple-element.133, pred[1024,2048]{1,0:T(8,128)(4,1)S(1)} %concatenate.28), kind=kOutput, calls=%fused_computation.76 | convolution fusion | flops 1673527296 | bytes 106717184 | tf_op jit(solution)/shard_map/hqk,qhd->khd/dot_general | solution.py:125
  2436.2 64.9 %multiply_reduce_fusion = (f32[6,1024]{1,0:T(8,128)S(1)}, f32[6,1024,2048]{2,1,0:T(8,128)}, f32[6,1024,2048]{2,1,0:T(8,128)}) fusion(f32[6,1024]{1,0:T(8,128)S(1)} %log_add_fusion, f32[6,1024,2048]{2,1,0:T(8,128)} %get-tuple-element.134, pred[1024,2048]{1,0:T(8,128)(4,1)S(1)} %concatenate.28, f32[6,1024,2048]{2,1,0:T(8,128)} %tile.19, ...), kind=kOutput, calls=%fused_computation.2 | convolution fusion | flops 1698686976 | bytes 205832192 | tf_op jit(solution)/shard_map/qhd,khd->hqk/dot_general | solution.py:128
  2501.1 79.4 %multiply_convert_fusion.3 = (bf16[6,1024,2048]{2,1,0:T(8,128)(2,1)}, bf16[6,1024,2048]{2,1,0:T(8,128)(2,1)}) fusion(f32[6,1024,2048]{2,1,0:T(8,128)} %get-tuple-element.78, f32[6,1024]{1,0:T(8,128)S(1)} %copy-done.36, f32[6,1024]{1,0:T(8,128)S(1)} %log_add_fusion.1, f32[6,1024,2048]{2,1,0:T(8,128)} %get-tuple-element.133, ...), kind=kLoop, calls=%fused_computation.5 | loop fusion | flops 150994944 | bytes 253853696 | tf_op jit(solution)/shard_map/convert_element_type | solution.py:133
  2594.3 33.5 %fusion.22 = f32[2048,6,64]{0,2,1:T(8,128)S(1)} fusion(bf16[1024,6,64]{0,2,1:T(8,128)(2,1)S(1)} %bitcast.205, f32[6,1024,2048]{2,1,0:T(8,128)} %tile.19, f32[6,1024]{1,0:T(8,128)S(1)} %log_add_fusion, f32[6,1024,2048]{2,1,0:T(8,128)} %get-tuple-element.134, pred[1024,2048]{1,0:T(8,128)(4,1)S(1)} %concatenate.28), kind=kOutput, calls=%fused_computation.75 | convolution fusion | flops 1673527296 | bytes 106717184 | tf_op jit(solution)/shard_map/hqk,qhd->khd/dot_general | solution.py:125
  2712.1 38.4 %all-gather.45.cloned.1.call-done = bf16[2048,1152]{0,1:T(8,128)(2,1)} async-done(((bf16[1024,1152]{0,1:T(8,128)(2,1)}), bf16[2048,1152]{0,1:T(8,128)(2,1)}) %all-gather.45.cloned.1.call-update) | async-done | bytes 4718608 | tf_op jit(solution)/shard_map/all_gather | solution.py:23
  2757.1 58.1 %all-gather.53.cloned.1.call-done = bf16[2048,1152]{0,1:T(8,128)(2,1)} async-done(((bf16[1024,1152]{0,1:T(8,128)(2,1)}), bf16[2048,1152]{0,1:T(8,128)(2,1)}) %all-gather.53.cloned.1.call-update) | async-done | bytes 4718608 | tf_op jit(solution)/shard_map/all_gather | solution.py:23
  2838.3 59.1 %reshape.262 = f32[6,1024,4,512]{3,2,1,0:T(4,128)} reshape(f32[6,1024,2048]{2,1,0:T(8,128)} %get-tuple-element.87) | data formatting | bytes 100663296 | tf_op jit(solution)/shard_map/reshape | solution.py:145
  2897.3 42.9 %reduce_sum.396 = f32[6,1024,512]{2,1,0:T(8,128)} reduce(f32[6,1024,4,512]{3,2,1,0:T(4,128)} %reshape.262, f32[]{:T(128)} %constant.48.clone.1), dimensions={2}, to_apply=%region_86.87 | reduce | flops 9437184 | bytes 62914564 | tf_op jit(solution)/shard_map/reduce_sum | solution.py:145
  2949.6 59.1 %reshape.264 = f32[6,1024,4,512]{3,2,1,0:T(4,128)} reshape(f32[6,1024,2048]{2,1,0:T(8,128)} %get-tuple-element.86) | data formatting | bytes 100663296 | tf_op jit(solution)/shard_map/reshape | solution.py:145
  3008.7 43.0 %reduce_sum.398 = f32[6,1024,512]{2,1,0:T(8,128)} reduce(f32[6,1024,4,512]{3,2,1,0:T(4,128)} %reshape.264, f32[]{:T(128)} %constant.48.clone.1), dimensions={2}, to_apply=%region_88.89 | reduce | flops 9437184 | bytes 62914564 | tf_op jit(solution)/shard_map/reduce_sum | solution.py:145
  3082.1 34.9 %all-reduce.5 = (f32[384]{0:T(512)}, f32[384]{0:T(512)}, f32[384]{0:T(512)}, f32[384]{0:T(512)}) all-reduce(f32[384]{0:T(512)S(1)} %add.416, f32[384]{0:T(512)S(1)} %add.417, f32[384]{0:T(512)S(1)} %add.422, f32[384]{0:T(512)S(1)} %add.423), channel_id=1, replica_groups=mesh['dp'=8,'row'=2,'col'=2] {'dp','col'}, use_global_device_ids=true, to_apply=%region_68.69 | all-reduce | flops 1536 | bytes 12288 | tf_op jit(solution)/shard_map/psum | solution.py:163
  (377 shorter events, 579.9 us)
Async XLA Ops:
  7.2 863.8 %copy-start = (bf16[1536,384]{1,0:T(8,128)(2,1)S(1)}, bf16[1536,384]{1,0:T(8,128)(2,1)}, u32[]{:S(2)}) copy-start(bf16[1536,384]{1,0:T(8,128)(2,1)} %param.25) | copy-start | bytes 3538948
  7.2 32.9 %all-gather.61.cloned.1.call-start = ((), (), s32[]{:S(2)}) async-start(), calls=%async_computation.59 | async-start | bytes 2359296 | tf_op jit(solution)/shard_map/all_gather | solution.py:19
  10.1 59.4 %all-gather.55.cloned.1.call-start = ((), (), s32[]{:S(2)}) async-start(), calls=%async_computation.56 | async-start | bytes 2359296 | tf_op jit(solution)/shard_map/all_gather | solution.py:19
  10.8 171.6 %reduce-scatter.30.cloned.1.call-start = ((), (), s32[]{:S(2)}) async-start(), calls=%async_computation.28 | async-start | bytes 14155776 | tf_op jit(solution)/shard_map/reduce_scatter | solution.py:39
  48.0 247.3 %reduce-scatter.22.cloned.1.call-start = ((), (), s32[]{:S(2)}) async-start(), calls=%async_computation.21 | async-start | bytes 14155776 | tf_op jit(solution)/shard_map/reduce_scatter | solution.py:39
  77.3 327.0 %all-gather.57.cloned.1.call-start = ((), (), s32[]{:S(2)}) async-start(), calls=%async_computation.57 | async-start | bytes 2359296 | tf_op jit(solution)/shard_map/all_gather | solution.py:241
  308.6 95.7 %all-gather.59.cloned.1.call-start = ((), (), s32[]{:S(2)}) async-start(), calls=%async_computation.58 | async-start | bytes 2359296 | tf_op jit(solution)/shard_map/all_gather | solution.py:240
  309.2 225.0 %all-gather.27.cloned.1.call-start = ((), (), s32[]{:S(2)}) async-start(), calls=%async_computation.22 | async-start | bytes 2359296 | tf_op jit(solution)/shard_map/all_gather | solution.py:23
  507.0 75.1 %reduce-scatter.24.cloned.1.call-start = ((), (), s32[]{:S(2)}) async-start(), calls=%async_computation.23 | async-start | bytes 4718592 | tf_op jit(solution)/shard_map/reduce_scatter | solution.py:52
  538.5 81.5 %all-gather.29.cloned.1.call-start = ((), (), s32[]{:S(2)}) async-start(), calls=%async_computation.24 | async-start | bytes 2359296 | tf_op jit(solution)/shard_map/all_gather | solution.py:19
  592.7 181.7 %reduce-scatter.26.cloned.1.call-start = ((), (), s32[]{:S(2)}) async-start(), calls=%async_computation.25 | async-start | bytes 18874368 | tf_op jit(solution)/shard_map/reduce_scatter | solution.py:39
  629.7 144.7 %copy-start.32 = (f32[1536]{0:T(1024)S(1)}, f32[1536]{0:T(1024)}, u32[]{:S(2)}) copy-start(f32[1536]{0:T(1024)} %param.24) | copy-start | bytes 18436
  629.8 241.2 %all-gather.31.cloned.1.call-start = ((), (), s32[]{:S(2)}) async-start(), calls=%async_computation.26 | async-start | bytes 9437184 | tf_op jit(solution)/shard_map/all_gather | solution.py:23
  790.5 132.0 %reduce-scatter.28.cloned.1.call-start = ((), (), s32[]{:S(2)}) async-start(), calls=%async_computation.27 | async-start | bytes 4718592 | tf_op jit(solution)/shard_map/reduce_scatter | solution.py:52
  878.9 91.2 %all-gather.39.cloned.1.call-start = ((), (), s32[]{:S(2)}) async-start(), calls=%async_computation.35 | async-start | bytes 2359296 | tf_op jit(solution)/shard_map/all_gather | solution.py:19
  942.8 179.9 %reduce-scatter.38.cloned.1.call-start = ((), (), s32[]{:S(2)}) async-start(), calls=%async_computation.36 | async-start | bytes 18874368 | tf_op jit(solution)/shard_map/reduce_scatter | solution.py:39
  978.0 234.8 %all-gather.41.cloned.1.call-start = ((), (), s32[]{:S(2)}) async-start(), calls=%async_computation.37 | async-start | bytes 9437184 | tf_op jit(solution)/shard_map/all_gather | solution.py:23
  1132.3 132.3 %reduce-scatter.40.cloned.1.call-start = ((), (), s32[]{:S(2)}) async-start(), calls=%async_computation.38 | async-start | bytes 4718592 | tf_op jit(solution)/shard_map/reduce_scatter | solution.py:52
  1221.0 83.8 %all-gather.43.cloned.1.call-start = ((), (), s32[]{:S(2)}) async-start(), calls=%async_computation.39 | async-start | bytes 2359296 | tf_op jit(solution)/shard_map/all_gather | solution.py:19
  1277.5 56.5 %all-gather.65.cloned.1.call-start = ((), (), s32[]{:S(2)}) async-start(), calls=%async_computation.61 | async-start | bytes 2359296 | tf_op jit(solution)/shard_map/all_gather | solution.py:240
  1280.7 82.7 %all-gather.63.cloned.1.call-start = ((), (), s32[]{:S(2)}) async-start(), calls=%async_computation.60 | async-start | bytes 2359296 | tf_op jit(solution)/shard_map/all_gather | solution.py:241
  1281.4 128.1 %reduce-scatter.42.cloned.1.call-start = ((), (), s32[]{:S(2)}) async-start(), calls=%async_computation.40 | async-start | bytes 4718592 | tf_op jit(solution)/shard_map/reduce_scatter | solution.py:39
  1309.1 305.8 %all-gather.33.cloned.1.call-start = ((), (), s32[]{:S(2)}) async-start(), calls=%async_computation.29 | async-start | bytes 2359296 | tf_op jit(solution)/shard_map/all_gather | solution.py:23
  1587.5 75.2 %reduce-scatter.32.cloned.1.call-start = ((), (), s32[]{:S(2)}) async-start(), calls=%async_computation.30 | async-start | bytes 4718592 | tf_op jit(solution)/shard_map/reduce_scatter | solution.py:52
  1619.2 81.5 %all-gather.35.cloned.1.call-start = ((), (), s32[]{:S(2)}) async-start(), calls=%async_computation.31 | async-start | bytes 2359296 | tf_op jit(solution)/shard_map/all_gather | solution.py:19
  1673.4 181.8 %reduce-scatter.34.cloned.1.call-start = ((), (), s32[]{:S(2)}) async-start(), calls=%async_computation.32 | async-start | bytes 18874368 | tf_op jit(solution)/shard_map/reduce_scatter | solution.py:39
  1710.4 144.7 %copy-start.33 = (f32[1536]{0:T(1024)S(1)}, f32[1536]{0:T(1024)}, u32[]{:S(2)}) copy-start(f32[1536]{0:T(1024)} %param.24) | copy-start | bytes 18436
  1710.4 241.3 %all-gather.37.cloned.1.call-start = ((), (), s32[]{:S(2)}) async-start(), calls=%async_computation.33 | async-start | bytes 9437184 | tf_op jit(solution)/shard_map/all_gather | solution.py:23
  1871.2 132.0 %reduce-scatter.36.cloned.1.call-start = ((), (), s32[]{:S(2)}) async-start(), calls=%async_computation.34 | async-start | bytes 4718592 | tf_op jit(solution)/shard_map/reduce_scatter | solution.py:52
  1959.6 90.2 %all-gather.47.cloned.1.call-start = ((), (), s32[]{:S(2)}) async-start(), calls=%async_computation.45 | async-start | bytes 2359296 | tf_op jit(solution)/shard_map/all_gather | solution.py:19
  2022.5 180.0 %reduce-scatter.50.cloned.1.call-start = ((), (), s32[]{:S(2)}) async-start(), calls=%async_computation.46 | async-start | bytes 18874368 | tf_op jit(solution)/shard_map/reduce_scatter | solution.py:39
  2057.8 234.8 %all-gather.49.cloned.1.call-start = ((), (), s32[]{:S(2)}) async-start(), calls=%async_computation.47 | async-start | bytes 9437184 | tf_op jit(solution)/shard_map/all_gather | solution.py:23
  2212.0 80.5 %copy-start.22 = (bf16[384,1536]{1,0:T(8,128)(2,1)S(1)}, bf16[384,1536]{1,0:T(8,128)(2,1)}, u32[]{:S(2)}) copy-start(bf16[384,1536]{1,0:T(8,128)(2,1)} %param.23) | copy-start | bytes 3538948
  2212.1 132.0 %reduce-scatter.52.cloned.1.call-start = ((), (), s32[]{:S(2)}) async-start(), calls=%async_computation.48 | async-start | bytes 4718592 | tf_op jit(solution)/shard_map/reduce_scatter | solution.py:52
  2300.5 84.1 %all-gather.51.cloned.1.call-start = ((), (), s32[]{:S(2)}) async-start(), calls=%async_computation.49 | async-start | bytes 2359296 | tf_op jit(solution)/shard_map/all_gather | solution.py:19
  2357.2 75.1 %reduce-scatter.54.cloned.1.call-start = ((), (), s32[]{:S(2)}) async-start(), calls=%async_computation.50 | async-start | bytes 4718592 | tf_op jit(solution)/shard_map/reduce_scatter | solution.py:39
  2388.8 268.0 %reduce-scatter.46.cloned.1.call-start = ((), (), s32[]{:S(2)}) async-start(), calls=%async_computation.42 | async-start | bytes 2359296 | tf_op jit(solution)/shard_map/reduce_scatter | solution.py:289
  2426.9 229.9 %reduce-scatter.44.cloned.1.call-start = ((), (), s32[]{:S(2)}) async-start(), calls=%async_computation.41 | async-start | bytes 2359296 | tf_op jit(solution)/shard_map/reduce_scatter | solution.py:286
  2501.1 79.4 %copy-start.27 = (bf16[1024,1,384]{0,2,1:T(8,128)(2,1)S(1)}, bf16[1024,1,384]{0,2,1:T(8,128)(2,1)}, u32[]{:S(2)}) copy-start(bf16[1024,1,384]{0,2,1:T(8,128)(2,1)} %get-tuple-element.98) | copy-start | bytes 2359300
  2593.8 79.8 %reduce-scatter.58.cloned.1.call-start = ((), (), s32[]{:S(2)}) async-start(), calls=%async_computation.52 | async-start | bytes 2359296 | tf_op jit(solution)/shard_map/reduce_scatter | solution.py:289
  2630.7 55.1 %reduce-scatter.56.cloned.1.call-start = ((), (), s32[]{:S(2)}) async-start(), calls=%async_computation.51 | async-start | bytes 2359296 | tf_op jit(solution)/shard_map/reduce_scatter | solution.py:286
  2643.7 106.7 %all-gather.45.cloned.1.call-start = ((), (), s32[]{:S(2)}) async-start(), calls=%async_computation.43 | async-start | bytes 7077888 | tf_op jit(solution)/shard_map/all_gather | solution.py:23
  2660.0 155.2 %all-gather.53.cloned.1.call-start = ((), (), s32[]{:S(2)}) async-start(), calls=%async_computation.53 | async-start | bytes 7077888 | tf_op jit(solution)/shard_map/all_gather | solution.py:23
  2689.2 452.3 %all-reduce.18.cloned.1.call-start = ((), (), s32[]{:S(2)}) async-start(), calls=%async_computation.62 | async-start | bytes 7077888 | tf_op jit(solution)/shard_map/psum | solution.py:154
  2712.1 103.2 %copy-start.28 = (bf16[1,2048,384]{2,1,0:T(8,128)(2,1)S(1)}, bf16[1,2048,384]{2,1,0:T(8,128)(2,1)}, u32[]{:S(2)}) copy-start(bf16[1,2048,384]{2,1,0:T(8,128)(2,1)} %all-gather.61.cloned.1.call-done) | copy-start | bytes 4718596
  2824.1 325.3 %reduce-scatter.48.cloned.1.call-start = ((), (), s32[]{:S(2)}) async-start(), calls=%async_computation.44 | async-start | bytes 4718592 | tf_op jit(solution)/shard_map/reduce_scatter | solution.py:52
  2831.3 320.8 %reduce-scatter.60.cloned.1.call-start = ((), (), s32[]{:S(2)}) async-start(), calls=%async_computation.54 | async-start | bytes 4718592 | tf_op jit(solution)/shard_map/reduce_scatter | solution.py:52
  2838.2 320.0 %reduce-scatter.62.cloned.1.call-start = ((), (), s32[]{:S(2)}) async-start(), calls=%async_computation.55 | async-start | bytes 6684672 | tf_op jit(solution)/shard_map/reduce_scatter | solution.py:168
  (55 other events, 1039.1 us)
Sparse Core Ops, SparseCore 0:
  10.2 29.8 all-gather.60
  42.3 27.1 all-gather.54
  71.8 110.6 reduce-scatter.29
  184.6 110.6 reduce-scatter.21
  308.7 27.1 all-gather.56
  337.9 27.1 all-gather.58
  507.1 27.0 all-gather.26
  538.7 43.4 reduce-scatter.23
  592.8 27.1 all-gather.28
  629.9 144.5 reduce-scatter.25
  790.6 80.3 all-gather.30
  879.0 43.4 reduce-scatter.27
  942.9 27.1 all-gather.38
  978.1 144.5 reduce-scatter.37
  1132.4 80.3 all-gather.40
  1221.2 43.4 reduce-scatter.39
  1277.6 27.1 all-gather.42
  1306.8 27.1 all-gather.64
  1336.2 27.1 all-gather.62
  1366.0 43.4 reduce-scatter.41
  1587.7 27.1 all-gather.32
  1619.3 43.4 reduce-scatter.31
  1673.5 27.1 all-gather.34
  1710.5 144.5 reduce-scatter.33
  1871.3 80.3 all-gather.36
  1959.7 43.4 reduce-scatter.35
  2022.6 27.1 all-gather.46
  2057.9 144.5 reduce-scatter.49
  2212.2 80.3 all-gather.48
  2300.6 43.4 reduce-scatter.51
  2357.4 27.1 all-gather.50
  2388.9 43.3 reduce-scatter.53
  2434.5 26.1 reduce-scatter.45
  2594.0 26.1 reduce-scatter.43
  2630.8 26.1 reduce-scatter.57
  2659.6 26.1 reduce-scatter.55
  2687.8 62.6 all-gather.44
  2752.6 62.6 all-gather.52
  2824.2 84.1 all-reduce.17
  2910.7 43.4 reduce-scatter.47
  2957.0 43.3 reduce-scatter.59
  3072.7 85.4 reduce-scatter.61
where the time goes:
time: 3180 us; the launch traced here: 3160 us
  waiting for transfers between devices  1830 us (58%)
  matrix products  537 us (17%)
  other arithmetic  411 us (13%)
  local copies, waits for them, and re-layouts  279 us (9%)
  blocking collectives  89 us (3%)
    reduce_scatter x8, waiting for transfers between devices, sum_over_rows(): lax.psum_scatter(partial_rows(jnp.int32(0), whole.shape[0] // lax.axis_si...  817 us
    all_gather x8, waiting for transfers between devices, gather_rows(): return lax.all_gather(local, 'row', axis=0, tiled=True)  473 us
    reduce_scatter x8, waiting for transfers between devices, sum_over_cols(): lax.psum_scatter(partial_rows(jnp.int32(0), whole.shape[0] // lax.axis_si...  261 us
    all_gather x8, waiting for transfers between devices, gather_cols(): return lax.all_gather(local, 'col', axis=0, tiled=True)  208 us
    reshape x2, local copies, waits for them, and re-layouts, fold_mask(): part.reshape(heads_here, block_rows, width // MASK_LEN, MASK_LEN).sum(2)  118 us
    dot_general x2, matrix products, score_table(): jnp.einsum('qhd,khd->hqk', query, keys_cat, preferred_element_type=jnp.fl...  117 us
    reduce_sum x2, other arithmetic, fold_mask(): part.reshape(heads_here, block_rows, width // MASK_LEN, MASK_LEN).sum(2)  85.9 us
    dot_general x2, matrix products, attend_back(): jnp.einsum('qhd,khd->hqk', grad_mixed, values_cat, preferred_element_type...  85.8 us
  transfers between devices with their start and end apart: 42, of which 34 were waited for; matrix products, arithmetic and copies ran while one was open for 23% of the time, Pallas kernels for 0%

commit v1 on v0

--- a/solution.py
+++ b/solution.py
@@ -1,6 +1,8 @@
 import jax
 import jax.numpy as jnp
 from jax import lax
+from jax.experimental import pallas as pl
+from jax.experimental.pallas import tpu as pltpu
 from jax.sharding import PartitionSpec as P
 
 D = 768
@@ -336,7 +338,529 @@
     )
 
 
+QBLOCK = 512
+PAIR = 2 * HDIM
+AXES = ("dp", "row", "col")
+
+
+def routes(groups):
+    def place(z, core, row, col):
+        return ((2 * z + core) * 2 + row) * 2 + col
+
+    spots = [
+        (z, core, row, col)
+        for z in range(groups // 2)
+        for core in range(2)
+        for row in range(2)
+        for col in range(2)
+    ]
+
+    def build(move):
+        return [(place(*spot), place(*move(*spot))) for spot in spots]
+
+    table = {
+        "keep": build(lambda z, k, r, c: (z, c, r, k)),
+        "turn": build(lambda z, k, r, c: (z, c, 1 - r, k)),
+        "core": build(lambda z, k, r, c: (z, 1 - k, r, c)),
+        "row": build(lambda z, k, r, c: (z, k, 1 - r, c)),
+        "col": build(lambda z, k, r, c: (z, k, r, 1 - c)),
+    }
+    bit = 1
+    while bit < groups // 2:
+        table[bit] = build(lambda z, k, r, c, bit=bit: (z ^ bit, k, r, c))
+        bit *= 2
+    return table
+
+
+def lane_head(shape, head):
+    lane = lax.broadcasted_iota(jnp.int32, shape, len(shape) - 1)
+    return (lane < HDIM) if head == 0 else (lane >= HDIM)
+
+
+def dot_nt(left, right):
+    return lax.dot_general(left, right, (((1,), (1,)), ((), ())), preferred_element_type=jnp.float32)
+
+
+def dot_nn(left, right):
+    return lax.dot_general(left, right, (((1,), (0,)), ((), ())), preferred_element_type=jnp.float32)
+
+
+def dot_tn(left, right):
+    return lax.dot_general(left, right, (((0,), (0,)), ((), ())), preferred_element_type=jnp.float32)
+
+
+def forward_kernel(core_ref, q_ref, k_ref, v_ref, mask_ref, o_ref, lse_ref):
+    core = core_ref[0]
+    step = pl.program_id(1)
+    prompt = core * PROMPT
+    here = lax.rem(step + 2 * core, 4) * QBLOCK
+
+    def run(starts):
+        query = q_ref[...]
+        outs, logs = [], []
+        for head in range(2):
+            q_head = jnp.where(lane_head(query.shape, head), query, jnp.zeros_like(query))
+            mask = mask_ref[head].astype(jnp.float32)
+            scores = [dot_nt(q_head, k_ref[pl.ds(s, QBLOCK), :]) for s in starts]
+            peak = scores[0]
+            for other in scores[1:]:
+                peak = jnp.maximum(peak, other)
+            peak = jnp.max(peak, axis=1, keepdims=True)
+            total = None
+            mixed = None
+            for s, score in zip(starts, scores):
+                expo = jnp.exp(score - peak)
+                total = expo if total is None else total + expo
+                low = (expo * mask).astype(jnp.bfloat16)
+                part = dot_nn(low, v_ref[pl.ds(s, QBLOCK), :])
+                mixed = part if mixed is None else mixed + part
+            total = jnp.sum(total, axis=1, keepdims=True)
+            outs.append(mixed / total)
+            logs.append(jnp.broadcast_to(peak + jnp.log(total), mixed.shape))
+        first = lane_head(outs[0].shape, 0)
+        o_ref[...] = jnp.where(first, outs[0], outs[1]).astype(jnp.bfloat16)
+        lse_ref[...] = jnp.where(first, logs[0], logs[1])
+
+    first_key = pl.multiple_of(prompt, QBLOCK)
+    second_key = pl.multiple_of(prompt + QBLOCK, QBLOCK)
+    own_key = pl.multiple_of(here, QBLOCK)
+
+    @pl.when(step < 2)
+    def _():
+        run([first_key, second_key])
+
+    @pl.when(step >= 2)
+    def _():
+        run([first_key, second_key, own_key])
+
+
+def backward_kernel(
+    core_ref,
+    q_ref,
+    k_ref,
+    v_ref,
+    do_ref,
+    o_ref,
+    lse_ref,
+    mask_ref,
+    dq_ref,
+    dk_ref,
+    dv_ref,
+    dm_ref,
+    dk_acc,
+    dv_acc,
+):
+    core = core_ref[0]
+    step = pl.program_id(1)
+    prompt = core * PROMPT
+    here = lax.rem(step + 2 * core, 4) * QBLOCK
+
+    @pl.when(step == 0)
+    def _():
+        dk_acc[...] = jnp.zeros_like(dk_acc)
+        dv_acc[...] = jnp.zeros_like(dv_acc)
+        dm_ref[...] = jnp.zeros_like(dm_ref)
+
+    def run(starts):
+        query = q_ref[...]
+        grad = do_ref[...]
+        blend = grad.astype(jnp.float32) * o_ref[...].astype(jnp.float32)
+        dqs = []
+        for head in range(2):
+            chosen = lane_head(query.shape, head)
+            q_head = jnp.where(chosen, query, jnp.zeros_like(query))
+            g_head = jnp.where(chosen, grad, jnp.zeros_like(grad))
+            delta = jnp.sum(jnp.where(chosen, blend, 0.0), axis=1, keepdims=True)
+            log_total = lse_ref[:, head * HDIM : head * HDIM + 1]
+            mask = mask_ref[head].astype(jnp.float32)
+            dq = None
+            for s in starts:
+                rows = pl.ds(s, QBLOCK)
+                prob = jnp.exp(dot_nt(q_head, k_ref[rows, :]) - log_total)
+                low = (prob * mask).astype(jnp.bfloat16)
+                dv_acc[rows, :] += dot_tn(low, g_head)
+                pull = dot_nt(g_head, v_ref[rows, :]) * prob
+                dm_ref[head] += pull
+                slope = (pull * mask - prob * delta).astype(jnp.bfloat16)
+                dk_acc[rows, :] += dot_tn(slope, q_head)
+                part = dot_nn(slope, k_ref[rows, :])
+                dq = part if dq is None else dq + part
+            dqs.append(dq)
+        dq_ref[...] = jnp.where(lane_head(dqs[0].shape, 0), dqs[0], dqs[1]).astype(jnp.bfloat16)
+
+    first_key = pl.multiple_of(prompt, QBLOCK)
+    second_key = pl.multiple_of(prompt + QBLOCK, QBLOCK)
+    own_key = pl.multiple_of(here, QBLOCK)
+
+    @pl.when(step < 2)
+    def _():
+        run([first_key, second_key])
+
+    @pl.when(step >= 2)
+    def _():
+        run([first_key, second_key, own_key])
+
+    @pl.when(step == 3)
+    def _():
+        dk_ref[...] = dk_acc[...].astype(jnp.bfloat16)
+        dv_ref[...] = dv_acc[...].astype(jnp.bfloat16)
+
+
+def attention_forward(core, joint, mask):
+    rows = joint.shape[0]
+    pairs = mask.shape[0] // 2
+    block = lambda p, j, core_ref: (lax.rem(j + 2 * core_ref[0], 4), p)
+    return pl.pallas_call(
+        forward_kernel,
+        grid_spec=pltpu.PrefetchScalarGridSpec(
+            num_scalar_prefetch=1,
+            grid=(pairs, 4),
+            in_specs=[
+                pl.BlockSpec((QBLOCK, PAIR), block),
+                pl.BlockSpec((rows, PAIR), lambda p, j, core_ref: (0, pairs + p)),
+                pl.BlockSpec((rows, PAIR), lambda p, j, core_ref: (0, 2 * pairs + p)),
+                pl.BlockSpec((2, MASK_LEN, MASK_LEN), lambda p, j, core_ref: (p, 0, 0)),
+            ],
+            out_specs=[
+                pl.BlockSpec((QBLOCK, PAIR), block),
+                pl.BlockSpec((QBLOCK, PAIR), block),
+            ],
+        ),
+        out_shape=[
+            jax.ShapeDtypeStruct((rows, pairs * PAIR), jnp.bfloat16),
+            jax.ShapeDtypeStruct((rows, pairs * PAIR), jnp.float32),
+        ],
+        compiler_params=pltpu.CompilerParams(
+            dimension_semantics=("arbitrary", "arbitrary"), vmem_limit_bytes=56 * 2**20
+        ),
+        cost_estimate=pl.CostEstimate(
+            flops=20 * pairs * 4 * 512 * 512 * 256, bytes_accessed=16 * 2**20, transcendentals=0
+        ),
+        name="attention_forward",
+    )(core, joint, joint, joint, mask)
+
+
+def attention_backward(core, joint, grad, mixed, log_total, mask):
+    rows = joint.shape[0]
+    pairs = mask.shape[0] // 2
+    block = lambda p, j, core_ref: (lax.rem(j + 2 * core_ref[0], 4), p)
+    whole = lambda p, j, core_ref: (0, p)
+    tables = lambda p, j, core_ref: (p, 0, 0)
+    return pl.pallas_call(
+        backward_kernel,
+        grid_spec=pltpu.PrefetchScalarGridSpec(
+            num_scalar_prefetch=1,
+            grid=(pairs, 4),
+            in_specs=[
+                pl.BlockSpec((QBLOCK, PAIR), block),
+                pl.BlockSpec((rows, PAIR), lambda p, j, core_ref: (0, pairs + p)),
+                pl.BlockSpec((rows, PAIR), lambda p, j, core_ref: (0, 2 * pairs + p)),
+                pl.BlockSpec((QBLOCK, PAIR), block),
+                pl.BlockSpec((QBLOCK, PAIR), block),
+                pl.BlockSpec((QBLOCK, PAIR), block),
+                pl.BlockSpec((2, MASK_LEN, MASK_LEN), tables),
+            ],
+            out_specs=[
+                pl.BlockSpec((QBLOCK, PAIR), block),
+                pl.BlockSpec((rows, PAIR), whole),
+                pl.BlockSpec((rows, PAIR), whole),
+                pl.BlockSpec((2, MASK_LEN, MASK_LEN), tables),
+            ],
+            scratch_shapes=[pltpu.VMEM((rows, PAIR), jnp.float32)] * 2,
+        ),
+        out_shape=[jax.ShapeDtypeStruct((rows, pairs * PAIR), jnp.bfloat16)] * 3
+        + [jax.ShapeDtypeStruct((2 * pairs, MASK_LEN, MASK_LEN), jnp.float32)],
+        compiler_params=pltpu.CompilerParams(
+            dimension_semantics=("arbitrary", "arbitrary"), vmem_limit_bytes=56 * 2**20
+        ),
+        cost_estimate=pl.CostEstimate(
+            flops=20 * pairs * 10 * 512 * 512 * 256, bytes_accessed=32 * 2**20, transcendentals=0
+        ),
+        name="attention_backward",
+    )(core, joint, joint, joint, grad, mixed, log_total, mask)
+
+
+def plus(left, right):
+    return (left.astype(jnp.float32) + right.astype(jnp.float32)).astype(jnp.bfloat16)
+
+
+def local_norm(values, gain, shift):
+    mean = jnp.mean(values, axis=-1, keepdims=True)
+    center = values - mean
+    scale = lax.rsqrt(jnp.mean(center * center, axis=-1, keepdims=True) + norm_eps)
+    normed = center * scale
+    return (normed, scale, normed * gain + shift)
+
+
+def local_norm_back(grad_out, normed, scale, gain):
+    scaled = grad_out * gain
+    first = jnp.mean(scaled, axis=-1, keepdims=True)
+    second = jnp.mean(scaled * normed, axis=-1, keepdims=True)
+    return scale * (scaled - first - normed * second)
+
+
+def on_chip(
+    tokens,
+    joint_weight,
+    joint_bias,
+    out_weight,
+    out_bias,
+    norm_gain,
+    norm_shift,
+    inner_weight,
+    inner_bias,
+    outer_weight,
+    outer_bias,
+    final_gain,
+    final_shift,
+    trained_gate_scores,
+    mask_noise,
+    cotangent,
+):
+    low = jnp.bfloat16
+    groups = lax.axis_size("dp")
+    table = routes(groups)
+    bits = [bit for bit in table if isinstance(bit, int)]
+    row = lax.axis_index("row")
+    group = lax.axis_index("dp")
+    core = lax.rem(group, 2)
+    height = lax.div(group, 2)
+    core_word = jnp.reshape(core, (1,)).astype(jnp.int32)
+    half_rows, width = tokens.shape[1:]
+    heads_here = trained_gate_scores.shape[0]
+    col_width = joint_weight.shape[2]
+    slim = col_width // 2
+    units = inner_weight.shape[1] // 2
+    taken = heads_here // 2
+
+    def send(value, way):
+        return lax.ppermute(value, AXES, table[way])
+
+    def pick(value, index, axis):
+        return lax.dynamic_index_in_dim(value, index, axis, keepdims=False)
+
+    def mine_first(value, axis):
+        parts = value.reshape(value.shape[:axis] + (2, value.shape[axis] // 2) + value.shape[axis + 1 :])
+        return (pick(parts, core, axis), pick(parts, 1 - core, axis))
+
+    def in_order(mine, other, axis):
+        first = jnp.where(core == 0, mine, other)
+        second = jnp.where(core == 0, other, mine)
+        return jnp.concatenate([first, second], axis)
+
+    def enter(whole):
+        return jnp.concatenate(
+            [send(pick(whole, row, 0), "keep"), send(pick(whole, 1 - row, 0), "turn")], 1
+        )
+
+    def leave(full):
+        kept = send(full[:, :width], "keep")
+        turned = send(full[:, width:], "turn")
+        lead = jnp.where(row == 0, kept, turned)
+        trail = jnp.where(row == 0, turned, kept)
+        return jnp.stack([lead, trail])
+
+    source = enter(tokens)
+    source_all = jnp.concatenate([source, send(source, "core")], 0)
+    joint_parts = joint_weight.transpose(1, 0, 2)
+    joint_mine = mine_first(joint_parts, 2)[0]
+    joint_mine = jnp.concatenate([joint_mine[:1] * 0.125, joint_mine[1:]], 0).astype(low)
+    joint_near = jnp.concatenate([joint_mine, send(joint_mine, "row")], 1)
+    joint_far = send(joint_near, "col")
+    joint_full = jnp.concatenate([joint_near, joint_far], 2)
+    joint_flat = joint_full.transpose(1, 0, 2).reshape(2 * width, 3 * col_width)
+
+    row_vec = jnp.stack([out_bias, norm_gain, norm_shift, outer_bias, final_gain, final_shift])
+    row_vec = jnp.concatenate([row_vec, send(row_vec, "row")], 1)
+    out_bias_all, gain_one, shift_one, outer_bias_all, gain_two, shift_two = (
+        row_vec[i] for i in range(6)
+    )
+    unit_mine, unit_other = mine_first(inner_bias, 0)
+    jb_mine = mine_first(joint_bias, 1)[0] * jnp.array([[0.125], [1.0]], jnp.float32)
+    col_vec = jnp.concatenate([unit_mine, unit_other, jb_mine.reshape(-1)])
+    col_far = send(col_vec, "col")
+    inner_bias_all = jnp.concatenate(
+        [unit_mine, col_far[:units], unit_other, col_far[units : 2 * units]]
+    )
+    jb_all = jnp.concatenate([jb_mine, col_far[2 * units :].reshape(2, slim)], 1)
+    joint_bias_all = jnp.concatenate([jb_all[0], jnp.zeros_like(jb_all[0]), jb_all[1]])
+
+    def chance(scores, noise):
+        return jax.nn.sigmoid((scores + jnp.log(noise) - jnp.log1p(-noise)) / relaxation_heat)
+
+    mask_mine = chance(
+        lax.dynamic_slice_in_dim(trained_gate_scores, core * taken, taken, 0),
+        lax.dynamic_slice_in_dim(mask_noise, core * taken, taken, 0),
+    ).astype(low)
+    mask = jnp.concatenate([mask_mine, send(mask_mine, "col")], 0)
+
+    joint = (jnp.dot(source_all, joint_flat, preferred_element_type=jnp.float32) + joint_bias_all).astype(low)
+    mixed, log_total = attention_forward(core_word, joint, mask)
+
+    ow = mine_first(out_weight, 0)[0]
+    ow = jnp.concatenate([ow, send(ow, "col")], 0)
+    ow = jnp.concatenate([ow, send(ow, "row")], 1)
+    out_full = jnp.concatenate([ow, send(ow, "core")], 0)
+    iw = mine_first(inner_weight, 1)[0]
+    iw = jnp.concatenate([iw, send(iw, "row")], 0)
+    iw = jnp.concatenate([iw, send(iw, "col")], 1)
+    inner_full = jnp.concatenate([iw, send(iw, "core")], 1)
+    uw = mine_first(outer_weight, 0)[0]
+    uw = jnp.concatenate([uw, send(uw, "col")], 0)
+    uw = jnp.concatenate([uw, send(uw, "row")], 1)
+    outer_full = jnp.concatenate([uw, send(uw, "core")], 0)
+    grad_result = enter(cotangent).astype(jnp.float32)
+
+    attended = jnp.concatenate([mixed[:half_rows], send(mixed[half_rows:], "core")], 1)
+    branch = jnp.dot(attended, out_full, preferred_element_type=jnp.float32) + out_bias_all
+    normed_one, scale_one, hidden = local_norm(
+        source.astype(jnp.float32) + branch, gain_one, shift_one
+    )
+    hidden_low = hidden.astype(low)
+    inner = jnp.dot(hidden_low, inner_full, preferred_element_type=jnp.float32) + inner_bias_all
+    open_part = 0.5 + 0.5 * lax.erf(inner * 0.7071067811865476)
+    active = (inner * open_part).astype(low)
+    bend = (open_part + inner * jnp.exp(-0.5 * inner * inner) * 0.3989422804014327).astype(low)
+    outer = jnp.dot(active, outer_full, preferred_element_type=jnp.float32) + outer_bias_all
+    normed_two, scale_two, result = local_norm(hidden + outer, gain_two, shift_two)
+    output = leave(result.astype(low))
+
+    grad_second = local_norm_back(grad_result, normed_two, scale_two, gain_two)
+    grad_outer = grad_second.astype(low)
+    grad_active = multiply(grad_outer, outer_full, True)
+    grad_inner = (grad_active * bend.astype(jnp.float32)).astype(low)
+    grad_hidden = multiply(grad_inner, inner_full, True) + grad_second
+    grad_first = local_norm_back(grad_hidden, normed_one, scale_one, gain_one)
+    grad_branch = grad_first.astype(low)
+    grad_attended = multiply(grad_branch, out_full, True).astype(low)
+    grad_mixed = jnp.concatenate(
+        [grad_attended[:, :col_width], send(grad_attended[:, col_width:], "core")], 0
+    )
+
+    grad_q, grad_k, grad_v, mask_part = attention_backward(
+        core_word, joint, grad_mixed, mixed, log_total, mask
+    )
+
+    def over_height(value):
+        for bit in bits:
+            value = plus(value, send(value, bit))
+        return value
+
+    both = units * 2
+    dw2_far = send(transpose_product(active[:, both:], grad_outer).astype(low), "core")
+    dw2 = plus(transpose_product(active[:, :both], grad_outer), dw2_far)
+    dw2 = plus(dw2[:units], send(dw2[units:], "col"))
+    dw2 = plus(dw2[:, :width], send(dw2[:, width:], "row"))
+    dw2 = over_height(dw2)
+    grad_outer_weight = in_order(dw2, send(dw2, "core"), 0).astype(jnp.float32)
+
+    dw1_far = send(transpose_product(hidden_low, grad_inner[:, both:]).astype(low), "core")
+    dw1 = plus(transpose_product(hidden_low, grad_inner[:, :both]), dw1_far)
+    dw1 = plus(dw1[:width], send(dw1[width:], "row"))
+    dw1 = plus(dw1[:, :units], send(dw1[:, units:], "col"))
+    dw1 = over_height(dw1)
+    grad_inner_weight = in_order(dw1, send(dw1, "core"), 1).astype(jnp.float32)
+
+    dwo_far = send(transpose_product(attended[:, col_width:], grad_branch).astype(low), "core")
+    dwo = plus(transpose_product(attended[:, :col_width], grad_branch), dwo_far)
+    dwo = plus(dwo[:slim], send(dwo[slim:], "col"))
+    dwo = plus(dwo[:, :width], send(dwo[:, width:], "row"))
+    dwo = over_height(dwo)
+    grad_out_weight = in_order(dwo, send(dwo, "core"), 0).astype(jnp.float32)
+
+    row_sums = jnp.stack(
+        [
+            jnp.sum(grad_branch.astype(jnp.float32), axis=0),
+            jnp.sum(grad_hidden * normed_one, axis=0),
+            jnp.sum(grad_hidden, axis=0),
+            jnp.sum(grad_outer.astype(jnp.float32), axis=0),
+            jnp.sum(grad_result * normed_two, axis=0),
+            jnp.sum(grad_result, axis=0),
+        ]
+    )
+    unit_sums = jnp.sum(grad_inner.astype(jnp.float32), axis=0).reshape(2, 2, units)
+    unit_near = in_order(unit_sums[0, 0], unit_sums[1, 0], 0)
+    unit_far = in_order(unit_sums[0, 1], unit_sums[1, 1], 0)
+    row_sums = row_sums[:, :width] + send(row_sums[:, width:], "row")
+    row_sums = row_sums + send(row_sums, "col")
+    unit_sum = unit_near + send(unit_far, "col")
+    unit_sum = unit_sum + send(unit_sum, "row")
+    vector = jnp.concatenate([row_sums.reshape(-1), unit_sum])
+    for way in ["core"] + bits:
+        vector = vector + send(vector, way)
+    row_grads = vector[: row_sums.size].reshape(row_sums.shape)
+    grad_inner_bias = vector[row_sums.size :]
+
+    grad_joint = jnp.concatenate([grad_q, grad_k, grad_v], 1)
+    grad_source = multiply(grad_joint, joint_flat, True)
+    grad_source = (
+        grad_source[:half_rows]
+        + send(grad_source[half_rows:].astype(low), "core").astype(jnp.float32)
+        + grad_first
+    )
+    grad_tokens = leave(grad_source.astype(low)).astype(jnp.float32)
+    dwj = transpose_product(source_all, grad_joint).astype(low).reshape(2, width, 3, 2, slim)
+    dwj = plus(dwj[0], send(dwj[1], "row"))
+    dwj = plus(dwj[:, :, 0], send(dwj[:, :, 1], "col"))
+    dwj = over_height(dwj)
+    grad_joint_weight = in_order(dwj, send(dwj, "core"), 2).astype(jnp.float32)
+    grad_joint_weight = grad_joint_weight * jnp.array([0.125, 1.0, 1.0], jnp.float32)[None, :, None]
+    joint_sums = jnp.sum(grad_joint.astype(jnp.float32), axis=0).reshape(3, 2, slim)
+    joint_sums = jnp.stack([joint_sums[0] * 0.125, joint_sums[2]])
+    joint_sums = joint_sums[:, 0] + send(joint_sums[:, 1], "col")
+    for way in ["row"] + bits:
+        joint_sums = joint_sums + send(joint_sums, way)
+    grad_joint_bias = in_order(joint_sums, send(joint_sums, "core"), 1)
+
+    heights = groups // 2
+    strip = MASK_LEN // (2 * groups)
+    pulled = mask_part[:taken] + send(mask_part[taken:].astype(low), "col").astype(jnp.float32)
+    pulled = pulled.astype(low).reshape(taken, heights, 2, 2, strip, MASK_LEN)
+    pulled = plus(pick(pulled, row, 3), send(pick(pulled, 1 - row, 3), "row"))
+    mine = pick(pulled, core, 2)
+    other = send(pick(pulled, 1 - core, 2), "core")
+    pulled = in_order(mine, other, 0)
+    span = heights
+    level = height
+    for bit in reversed(bits):
+        parts = pulled.reshape(heads_here, 2, span // 2, strip, MASK_LEN)
+        upper = lax.div(level, bit)
+        pulled = plus(pick(parts, upper, 1), send(pick(parts, 1 - upper, 1), bit))
+        level = lax.rem(level, bit)
+        span = span // 2
+    pulled = pulled.reshape(heads_here, strip, MASK_LEN).astype(jnp.float32)
+    first_row = (group * 2 + row) * strip
+    gate = chance(
+        lax.dynamic_slice_in_dim(trained_gate_scores, first_row, strip, 1),
+        lax.dynamic_slice_in_dim(mask_noise, first_row, strip, 1),
+    )
+    grad_mask = pulled * gate * (1.0 - gate) / relaxation_heat
+
+    return (
+        output,
+        grad_tokens,
+        grad_joint_weight,
+        grad_joint_bias,
+        grad_out_weight,
+        row_grads[0],
+        row_grads[1],
+        row_grads[2],
+        grad_inner_weight,
+        grad_inner_bias,
+        grad_outer_weight,
+        row_grads[3],
+        row_grads[4],
+        row_grads[5],
+        grad_mask,
+    )
+
+
 def solution(mesh):
+    sizes = dict(mesh.shape)
+    heights = sizes["dp"] // 2
+    square = sizes["row"] == 2 and sizes["col"] == 2
+    paired = sizes["dp"] % 2 == 0 and heights & (heights - 1) == 0 and MASK_LEN % (2 * sizes["dp"]) == 0
+    body = on_chip if square and paired else on_device
     placed = (
         P(None, ("dp", "col"), "row"),
         P("row", None, "col"),
@@ -356,7 +880,7 @@
         P(None, ("dp", "col"), "row"),
     )
     return jax.shard_map(
-        on_device,
+        body,
         mesh=mesh,
         in_specs=placed,
         out_specs=(

time: 3180 us -> 670 us (0.21)
  waiting for transfers between devices: 1830 us -> 252 us
  matrix products: 537 us -> 108 us
  other arithmetic: 411 us -> 64.8 us
  local copies, waits for them, and re-layouts: 279 us -> 58.6 us
  Pallas kernels: 0 us -> 102 us
  blocking collectives: 89 us -> 0 us
  starting transfers between devices: 4.43 us -> 74.8 us
    reduce_scatter x21 -> x0, waiting for transfers between devices: 1090 us -> none  [the longest x8 817 us: sum_over_rows(): lax.psum_scatter(partial_rows(jnp.int32(0), whole.shape[0] // lax.axis_si...]
    all_gather x20 -> x0, waiting for transfers between devices: 734 us -> none  [the longest x8 473 us: gather_rows(): return lax.all_gather(local, 'row', axis=0, tiled=True)]
    dot_general x20 -> x4, matrix products: 447 us -> 34.9 us  [the longest x1 13.3 us: on_chip(): jnp.dot(hidden_low, inner_full, preferred_element_type=jnp.float32)]
    ppermute x0 -> x66, waiting for transfers between devices: none -> 252 us  [send(): return lax.ppermute(value, AXES, table[way])]
    reduce_sum x23 -> x6, other arithmetic: 194 us -> 8.19 us  [the longest x1 3.08 us: on_chip(): jnp.sum(grad_outer.astype(jnp.float32), axis=0)]
    convert_element_type x25 -> x26, other arithmetic: 166 us -> 25.6 us  [the longest x18 12.2 us: plus(): (left.astype(jnp.float32) + right.astype(jnp.float32)).astype(jnp.bfloat16)]
    reshape x3 -> x5, local copies, waits for them, and re-layouts: 120 us -> 0.19 us  [the longest x2 0.09 us: mine_first(): value.reshape(value.shape[:axis] + (2, value.shape[axis] // 2) + value.sh...]
    pallas_call x0 -> x2, Pallas kernels: none -> 102 us  [the longest x1 66.8 us: attention_backward(): pl.pallas_call(backward_kernel, grid_spec=pltpu.PrefetchScalarGridSpec(nu...]
  transfers between devices with their start and end apart: 42 -> 66, of which waited for: 34 -> 22; matrix products, arithmetic and copies ran while one was open for 23% -> 26% of each run, Pallas kernels for 0% -> 15%
where the time goes in v1:
time: 670 us; the launch traced here: 662 us
  waiting for transfers between devices  252 us (38%)
  matrix products  108 us (16%)
  Pallas kernels  102 us (15%)
  starting transfers between devices  74.8 us (11%)
  other arithmetic  64.8 us (10%)
  local copies, waits for them, and re-layouts  58.6 us (9%)
    ppermute x66, waiting for transfers between devices, send(): return lax.ppermute(value, AXES, table[way])  252 us
    ppermute x66, starting transfers between devices, send(): return lax.ppermute(value, AXES, table[way])  74.8 us
    pallas_call x1, Pallas kernels, attention_backward(): pl.pallas_call(backward_kernel, grid_spec=pltpu.PrefetchScalarGridSpec(nu...  66.8 us
    dot_general x4, matrix products, multiply(): lax.dot_general(block, weight, (((1,), (1,)), ((), ())), preferred_elemen...  39.2 us
    pallas_call x1, Pallas kernels, attention_forward(): pl.pallas_call(forward_kernel, grid_spec=pltpu.PrefetchScalarGridSpec(num...  35 us
    dot_general x7, matrix products, transpose_product(): lax.dot_general(left, right, (((0,), (0,)), ((), ())), preferred_element_...  33.5 us
    unnamed x136, local copies, waits for them, and re-layouts  21.7 us
  transfers between devices with their start and end apart: 66, of which 22 were waited for; matrix products, arithmetic and copies ran while one was open for 26% of the time, Pallas kernels for 15%

profile of v1, /device:TPU:0, one launch (start us, length us, event | category | flops | bytes accessed | tf_op | source)
XLA Modules:
  0.0 662.4 jit_solution(3326623006620183102)
XLA Ops:
  0.7 2.6 copy.67
  4.9 3.0 collective-permute-start.3
  11.8 3.5 constant_dynamic-slice_fusion.6
  19.5 7.4 %collective-permute-start = (bf16[1024,384]{0,1:T(8,128)(2,1)}, bf16[1024,384]{0,1:T(8,128)(2,1)}, u32[]{:S(2)}, u32[]{:S(2)}) collective-permute-start(bf16[1024,384]{0,1:T(8,128)(2,1)} %bitcast), channel_id=1, source_target_pairs={{0,0},{1,4},{2,2},{3,6},{4,1},{5,5},{6,3},{7,7},{8,8},{9,12},{10,1... | collective-permute-start | bytes 2359304 | tf_op jit(solution)/shard_map/ppermute | solution.py:637
  26.9 4.9 divide_convert_fusion
  40.4 7.4 %collective-permute-done.1 = bf16[1024,384]{0,1:T(8,128)(2,1)} collective-permute-done((bf16[1024,384]{0,1:T(8,128)(2,1)}, bf16[1024,384]{0,1:T(8,128)(2,1)}, u32[]{:S(2)}, u32[]{:S(2)}) %collective-permute-start.1) | collective-permute-done | bytes 786464 | tf_op jit(solution)/shard_map/ppermute | solution.py:637
  50.7 26.9 %collective-permute-done.5 = f32[1920]{0:T(1024)S(1)} collective-permute-done((f32[1920]{0:T(1024)S(1)}, f32[1920]{0:T(1024)S(1)}, u32[]{:S(2)}, u32[]{:S(2)}) %collective-permute-start.5) | collective-permute-done | bytes 7712 | tf_op jit(solution)/shard_map/ppermute | solution.py:637
  82.8 10.6 %collective-permute-done.15 = bf16[768,384]{1,0:T(8,128)(2,1)S(1)} collective-permute-done((bf16[768,384]{1,0:T(8,128)(2,1)}, bf16[768,384]{1,0:T(8,128)(2,1)S(1)}, u32[]{:S(2)}, u32[]{:S(2)}) %collective-permute-start.15) | collective-permute-done | bytes 589856 | tf_op jit(solution)/shard_map/ppermute | solution.py:637
  96.1 16.4 %collective-permute-done.4 = bf16[3,768,192]{1,2,0:T(8,128)(2,1)} collective-permute-done((bf16[3,768,192]{1,2,0:T(8,128)(2,1)}, bf16[3,768,192]{1,2,0:T(8,128)(2,1)}, u32[]{:S(2)}, u32[]{:S(2)}) %collective-permute-start.4) | collective-permute-done | bytes 884768 | tf_op jit(solution)/shard_map/ppermute | solution.py:637
  114.4 4.0 pad_maximum_fusion.3.mask_ref
  118.4 18.3 %collective-permute-done.13 = bf16[768,768]{1,0:T(8,128)(2,1)} collective-permute-done((bf16[768,768]{1,0:T(8,128)(2,1)}, bf16[768,768]{1,0:T(8,128)(2,1)}, u32[]{:S(2)}, u32[]{:S(2)}) %collective-permute-start.13) | collective-permute-done | bytes 1179680 | tf_op jit(solution)/shard_map/ppermute | solution.py:637
  136.7 3.0 pad_maximum_fusion.4
  139.7 8.9 %add_convert_fusion.q_ref.k_ref.v_ref = bf16[2048,1152]{1,0:T(8,128)(2,1)} fusion(bf16[768,1152]{0,1:T(8,128)(2,1)S(1)} %bitcast.108, f32[1152]{0:T(1024)S(1)} %pad_maximum_fusion.29, bf16[1024,768]{0,1:T(8,128)(2,1)} %collective-permute-done.2, bf16[1024,768]{0,1:T(8,128)(2,1)} %constant_dynamic-update-slice_fusion), kind=kOutput, calls=%fused_computation.11 | convolution fusion | flops 3634888704 | bytes 9638400 | tf_op jit(solution)/shard_map/dot_general | solution.py:697
  148.6 35.0 %attention_forward.1 = (bf16[2048,384]{1,0:T(8,128)(2,1)}, f32[2048,384]{1,0:T(8,128)}) custom-call(s32[1]{0:T(128)} %bitcast.2.core_ref, bf16[2048,1152]{1,0:T(8,128)(2,1)} %add_convert_fusion.q_ref.k_ref.v_ref, bf16[2048,1152]{1,0:T(8,128)(2,1)} %add_convert_fusion.q_ref.k_ref.v_ref, bf16[2048,1152]{1,0:T(8,128)(2,1)} %add_convert_fusion.q_ref.k_ref.v_ref, ...), custom_call_target="tpu_custom_call" | custom-call | flops 16106127360 | bytes 16777216 | tf_op jit(solution)/shard_map/attention_forward/pallas_call | solution.py:513
  183.7 2.6 fusion.71
  198.0 3.6 fusion.74
  203.1 13.3 %multiply_convert_fusion.1 = (bf16[1024,3072]{1,0:T(8,128)(2,1)}, f32[1024,3072]{1,0:T(8,128)}) fusion(f32[3072]{0:T(1024)S(1)} %pad_maximum_fusion.27, bf16[1024,768]{0,1:T(8,128)(2,1)S(1)} %fusion.24, bf16[768,1536]{1,0:T(8,128)(2,1)} %collective-permute-done.14, bf16[768,768]{1,0:T(8,128)(2,1)} %collective-permute-done.13, ...), kind=kOutput, calls=%fused_computation.8 | convolution fusion | flops 4869586944 | bytes 25178112 | tf_op jit(solution)/shard_map/dot_general | solution.py:720
  216.4 9.1 %fusion.75 = (f32[1024]{0:T(1024)S(1)}, f32[1024,768]{0,1:T(8,128)S(1)}) fusion(f32[768]{0:T(1024)S(1)} %get-tuple-element.81, bf16[1024,3072]{1,0:T(8,128)(2,1)} %get-tuple-element.147, bf16[1536,768]{1,0:T(8,128)(2,1)S(1)} %collective-permute-done.17, bf16[1536,384]{1,0:T(8,128)(2,1)} %collective-permute-done.16, bf16[768,384]{1,0:T(8,128)(2,1)S(1)} %copy-done.23, ...), kind=kOutput, calls=%fused_computation.228 | convolution fusion | flops 4856216576 | bytes 17323008 | tf_op jit(solution)/shard_map/dot_general | solution.py:724
  227.4 3.1 convert_reduce_fusion.3
  230.5 4.1 convolution_convert_fusion
  235.7 18.5 %convert_reduce_fusion = (f32[3072]{0:T(1024)S(1)}, bf16[1024,3072]{1,0:T(8,128)(2,1)}) fusion(f32[1024,3072]{1,0:T(8,128)S(1)} %bitcast.115, f32[3072]{0:T(1024)S(1)} %pad_maximum_fusion.27, bf16[1024,768]{0,1:T(8,128)(2,1)S(1)} %get-tuple-element.95, bf16[1536,768]{1,0:T(8,128)(2,1)S(1)} %collective-permute-done.17, ...), kind=kOutput, calls=%fused_computation.6 | convolution fusion | flops 4897895424 | bytes 25190400 | tf_op jit(solution)/shard_map/dot_general | solution.py:30
  254.3 6.5 convolution_convert_fusion.1
  260.9 11.1 %multiply_reduce_fusion = (f32[768]{0:T(1024)S(1)}, f32[1024]{0:T(1024)S(1)}, f32[1024]{0:T(1024)S(1)}, f32[768]{0:T(1024)S(1)}, f32[1024,768]{0,1:T(8,128)S(1)}) fusion(f32[1024,768]{0,1:T(8,128)S(1)} %get-tuple-element.146, f32[1024]{0:T(1024)S(1)} %add_rsqrt_fusion.1, f32[1024]{0:T(1024)S(1)} %broadcast_multiply_fusion.5, ...), kind=kOutput, calls=%fused_computation.44 | convolution fusion | flops 4867223552 | bytes 22065152 | tf_op jit(solution)/shard_map/dot_general | solution.py:30
  280.3 3.3 convolution_convert_fusion.4
  284.2 3.1 convolution_convert_fusion.3
  291.2 2.6 collective-permute-start.48
  295.1 7.4 %collective-permute-start.18 = (bf16[1024,384]{0,1:T(8,128)(2,1)}, bf16[1024,384]{0,1:T(8,128)(2,1)}, u32[]{:S(2)}, u32[]{:S(2)}) collective-permute-start(bf16[1024,384]{0,1:T(8,128)(2,1)} %get-tuple-element.115), channel_id=1, source_target_pairs={{0,0},{1,4},{2,2},{3,6},{4,1},{5,5},{6,3},{7,7},{8,8},{9,12},{10,1... | collective-permute-start | bytes 2359304 | tf_op jit(solution)/shard_map/ppermute | solution.py:637
  308.4 66.8 %attention_backward.1 = (bf16[2048,384]{1,0:T(8,128)(2,1)}, bf16[2048,384]{1,0:T(8,128)(2,1)}, bf16[2048,384]{1,0:T(8,128)(2,1)}, f32[6,512,512]{2,1,0:T(8,128)}) custom-call(s32[1]{0:T(128)} %bitcast.2.core_ref, bf16[2048,1152]{1,0:T(8,128)(2,1)} %add_convert_fusion.q_ref.k_ref.v_ref, bf16[2048,1152]{1,0:T(8,128)(2,1)} %add_convert_fusion.q_ref.k_ref.v_ref, ...), custom_call_target="tpu_custom_call" | custom-call | flops 40265318400 | bytes 33554432 | tf_op jit(solution)/shard_map/attention_backward/pallas_call | solution.py:549
  380.7 6.5 fusion.76
  389.5 7.5 %convolution_convert_fusion.2 = bf16[768,1152]{1,0:T(8,128)(2,1)S(1)} fusion(bf16[2048,1152]{1,0:T(8,128)(2,1)} %copy-done.6, bf16[1024,768]{0,1:T(8,128)(2,1)} %collective-permute-done.2, bf16[1024,768]{0,1:T(8,128)(2,1)} %constant_dynamic-update-slice_fusion), kind=kOutput, calls=%fused_computation.24 | convolution fusion | flops 3631054848 | bytes 9633792 | tf_op jit(solution)/shard_map/dot_general | solution.py:63
  409.2 18.7 %collective-permute-done.38 = bf16[192,384]{1,0:T(8,128)(2,1)S(1)} collective-permute-done((bf16[192,384]{1,0:T(8,128)(2,1)S(1)}, bf16[192,384]{1,0:T(8,128)(2,1)S(1)}, u32[]{:S(2)}, u32[]{:S(2)}) %collective-permute-start.38) | collective-permute-done | bytes 147488 | tf_op jit(solution)/shard_map/ppermute | solution.py:637
  433.4 3.3 slice.415
  436.7 3.4 slice.416
  440.1 2.8 copy.76
  444.5 9.5 %collective-permute-done.40 = bf16[192,384]{1,0:T(8,128)(2,1)S(1)} collective-permute-done((bf16[192,384]{1,0:T(8,128)(2,1)S(1)}, bf16[192,384]{1,0:T(8,128)(2,1)S(1)}, u32[]{:S(2)}, u32[]{:S(2)}) %collective-permute-start.40) | collective-permute-done | bytes 147488 | tf_op jit(solution)/shard_map/ppermute | solution.py:637
  460.0 28.2 %collective-permute-done.27 = bf16[384,3,192]{0,2,1:T(8,128)(2,1)S(1)} collective-permute-done((bf16[384,3,192]{0,2,1:T(8,128)(2,1)S(1)}, bf16[384,3,192]{0,2,1:T(8,128)(2,1)S(1)}, u32[]{:S(2)}, u32[]{:S(2)}) %collective-permute-start.27) | collective-permute-done | bytes 442400 | tf_op jit(solution)/shard_map/ppermute | solution.py:637
  492.7 5.1 add_convert_fusion.1
  503.2 5.1 add_convert_fusion.2
  509.5 15.9 %collective-permute-done.29 = bf16[384,3,192]{0,2,1:T(8,128)(2,1)S(1)} collective-permute-done((bf16[384,3,192]{0,2,1:T(8,128)(2,1)S(1)}, bf16[384,3,192]{0,2,1:T(8,128)(2,1)S(1)}, u32[]{:S(2)}, u32[]{:S(2)}) %collective-permute-start.29) | collective-permute-done | bytes 442400 | tf_op jit(solution)/shard_map/ppermute | solution.py:637
  529.1 13.3 %collective-permute-start.63 = (bf16[3,4,32,512]{3,2,1,0:T(8,128)(2,1)S(1)}, bf16[3,4,32,512]{3,2,1,0:T(8,128)(2,1)}, u32[]{:S(2)}, u32[]{:S(2)}) collective-permute-start(bf16[3,4,32,512]{3,2,1,0:T(8,128)(2,1)S(1)} %dynamic-slice_bitcast_fusion.1), channel_id=1, source_target_pairs={{0,4},{1,5},{2,6},{3,7},{4,0},{5,1},{6,2},{7,3},{8,12},{9,13},{10,... | collective-permute-start | bytes 1179656 | tf_op jit(solution)/shard_map/ppermute | solution.py:637
  549.3 5.2 collective-permute-done.50
  556.2 10.7 %collective-permute-done.57 = bf16[768,384]{1,0:T(8,128)(2,1)S(1)} collective-permute-done((bf16[768,384]{1,0:T(8,128)(2,1)S(1)}, bf16[768,384]{1,0:T(8,128)(2,1)S(1)}, u32[]{:S(2)}, u32[]{:S(2)}) %collective-permute-start.57) | collective-permute-done | bytes 589856 | tf_op jit(solution)/shard_map/ppermute | solution.py:637
  568.3 2.9 collective-permute-done.51
  573.5 18.2 %collective-permute-done.58 = bf16[768,384]{1,0:T(8,128)(2,1)S(1)} collective-permute-done((bf16[768,384]{1,0:T(8,128)(2,1)S(1)}, bf16[768,384]{1,0:T(8,128)(2,1)S(1)}, u32[]{:S(2)}, u32[]{:S(2)}) %collective-permute-start.58) | collective-permute-done | bytes 589856 | tf_op jit(solution)/shard_map/ppermute | solution.py:637
  593.9 10.5 %collective-permute-done.52 = bf16[384,768]{1,0:T(8,128)(2,1)} collective-permute-done((bf16[384,768]{1,0:T(8,128)(2,1)S(1)}, bf16[384,768]{1,0:T(8,128)(2,1)}, u32[]{:S(2)}, u32[]{:S(2)}) %collective-permute-start.52) | collective-permute-done | bytes 589856 | tf_op jit(solution)/shard_map/ppermute | solution.py:637
  608.1 32.7 %collective-permute-done.59 = bf16[768,384]{1,0:T(8,128)(2,1)} collective-permute-done((bf16[768,384]{1,0:T(8,128)(2,1)S(1)}, bf16[768,384]{1,0:T(8,128)(2,1)}, u32[]{:S(2)}, u32[]{:S(2)}) %collective-permute-start.59) | collective-permute-done | bytes 589856 | tf_op jit(solution)/shard_map/ppermute | solution.py:637
  642.1 10.2 %collective-permute-done.53 = bf16[384,768]{1,0:T(8,128)(2,1)S(1)} collective-permute-done((bf16[384,768]{1,0:T(8,128)(2,1)S(1)}, bf16[384,768]{1,0:T(8,128)(2,1)S(1)}, u32[]{:S(2)}, u32[]{:S(2)}) %collective-permute-start.53) | collective-permute-done | bytes 589856 | tf_op jit(solution)/shard_map/ppermute | solution.py:637
  652.6 3.9 collective-permute-done.65
  (395 shorter events, 139.8 us)
Async XLA Ops:
  4.9 29.3 %collective-permute-start.3 = (bf16[3,384,192]{1,2,0:T(8,128)(2,1)}, bf16[3,384,192]{1,2,0:T(8,128)(2,1)}, u32[]{:S(2)}, u32[]{:S(2)}) collective-permute-start(bf16[3,384,192]{1,2,0:T(8,128)(2,1)} %pad_maximum_fusion.22), channel_id=1, source_target_pairs={{0,2},{1,3},{2,0},{3,1},{4,6},{5,7},{6,4},{7,5},{8,10},{9,11},{10,... | collective-permute-start | bytes 1327112 | tf_op jit(solution)/shard_map/ppermute | solution.py:637
  11.7 65.9 %collective-permute-start.12 = (bf16[384,768]{1,0:T(8,128)(2,1)S(1)}, bf16[384,768]{1,0:T(8,128)(2,1)}, u32[]{:S(2)}, u32[]{:S(2)}) collective-permute-start(bf16[384,768]{1,0:T(8,128)(2,1)S(1)} %bitcast.97), channel_id=1, source_target_pairs={{0,2},{1,3},{2,0},{3,1},{4,6},{5,7},{6,4},{7,5},{8,10},{9,11},{10,... | collective-permute-start | bytes 1769480 | tf_op jit(solution)/shard_map/ppermute | solution.py:637
  16.5 31.4 %collective-permute-start.1 = (bf16[1024,384]{0,1:T(8,128)(2,1)}, bf16[1024,384]{0,1:T(8,128)(2,1)}, u32[]{:S(2)}, u32[]{:S(2)}) collective-permute-start(bf16[1024,384]{0,1:T(8,128)(2,1)} %bitcast.111), channel_id=1, source_target_pairs={{0,2},{1,6},{2,0},{3,4},{4,3},{5,7},{6,1},{7,5},{8,10},{9,14},{10,... | collective-permute-start | bytes 2359304 | tf_op jit(solution)/shard_map/ppermute | solution.py:637
  19.5 18.8 %collective-permute-start = (bf16[1024,384]{0,1:T(8,128)(2,1)}, bf16[1024,384]{0,1:T(8,128)(2,1)}, u32[]{:S(2)}, u32[]{:S(2)}) collective-permute-start(bf16[1024,384]{0,1:T(8,128)(2,1)} %bitcast), channel_id=1, source_target_pairs={{0,0},{1,4},{2,2},{3,6},{4,1},{5,5},{6,3},{7,7},{8,8},{9,12},{10,1... | collective-permute-start | bytes 2359304 | tf_op jit(solution)/shard_map/ppermute | solution.py:637
  31.8 82.6 %collective-permute-start.6 = (bf16[3,512,512]{2,1,0:T(8,128)(2,1)S(1)}, bf16[3,512,512]{2,1,0:T(8,128)(2,1)}, u32[]{:S(2)}, u32[]{:S(2)}) collective-permute-start(bf16[3,512,512]{2,1,0:T(8,128)(2,1)S(1)} %divide_convert_fusion), channel_id=1, source_target_pairs={{0,1},{1,0},{2,3},{3,2},{4,5},{5,4},{6,7},{7,6},{8,9},{9,8},{10,11... | collective-permute-start | bytes 4718600 | tf_op jit(solution)/shard_map/ppermute | solution.py:637
  34.2 43.4 %collective-permute-start.5 = (f32[1920]{0:T(1024)S(1)}, f32[1920]{0:T(1024)S(1)}, u32[]{:S(2)}, u32[]{:S(2)}) collective-permute-start(f32[1920]{0:T(1024)S(1)} %pad_maximum_fusion.28), channel_id=1, source_target_pairs={{0,1},{1,0},{2,3},{3,2},{4,5},{5,4},{6,7},{7,6},{8,9},{9,8},{10,11... | collective-permute-start | bytes 23048 | tf_op jit(solution)/shard_map/ppermute | solution.py:637
  38.3 42.5 %collective-permute-start.8 = (bf16[192,384]{1,0:T(8,128)(2,1)S(1)}, bf16[192,384]{1,0:T(8,128)(2,1)S(1)}, u32[]{:S(2)}, u32[]{:S(2)}) collective-permute-start(bf16[192,384]{1,0:T(8,128)(2,1)S(1)} %dynamic-slice_bitcast_fusion.3), channel_id=1, source_target_pairs={{0,1},{1,0},{2,3},{3,2},{4,5},{5,4},{6,7},{7,6},{8,9},{9,8},{10,11... | collective-permute-start | bytes 442376 | tf_op jit(solution)/shard_map/ppermute | solution.py:637
  47.8 45.6 %collective-permute-start.15 = (bf16[768,384]{1,0:T(8,128)(2,1)}, bf16[768,384]{1,0:T(8,128)(2,1)S(1)}, u32[]{:S(2)}, u32[]{:S(2)}) collective-permute-start(bf16[768,384]{1,0:T(8,128)(2,1)} %dynamic-slice_bitcast_fusion), channel_id=1, source_target_pairs={{0,1},{1,0},{2,3},{3,2},{4,5},{5,4},{6,7},{7,6},{8,9},{9,8},{10,11... | collective-permute-start | bytes 1769480 | tf_op jit(solution)/shard_map/ppermute | solution.py:637
  77.6 34.9 %collective-permute-start.4 = (bf16[3,768,192]{1,2,0:T(8,128)(2,1)}, bf16[3,768,192]{1,2,0:T(8,128)(2,1)}, u32[]{:S(2)}, u32[]{:S(2)}) collective-permute-start(bf16[3,768,192]{1,2,0:T(8,128)(2,1)} %pad_maximum_fusion.15), channel_id=1, source_target_pairs={{0,1},{1,0},{2,3},{3,2},{4,5},{5,4},{6,7},{7,6},{8,9},{9,8},{10,11... | collective-permute-start | bytes 2654216 | tf_op jit(solution)/shard_map/ppermute | solution.py:637
  77.6 62.1 %collective-permute-start.2 = (bf16[1024,768]{0,1:T(8,128)(2,1)}, bf16[1024,768]{0,1:T(8,128)(2,1)}, u32[]{:S(2)}, u32[]{:S(2)}) collective-permute-start(bf16[1024,768]{0,1:T(8,128)(2,1)} %constant_dynamic-update-slice_fusion), channel_id=1, source_target_pairs={{0,4},{1,5},{2,6},{3,7},{4,0},{5,1},{6,2},{7,3},{8,12},{9,13},{10,... | collective-permute-start | bytes 4718600 | tf_op jit(solution)/shard_map/ppermute | solution.py:637
  80.8 55.9 %collective-permute-start.13 = (bf16[768,768]{1,0:T(8,128)(2,1)}, bf16[768,768]{1,0:T(8,128)(2,1)}, u32[]{:S(2)}, u32[]{:S(2)}) collective-permute-start(bf16[768,768]{1,0:T(8,128)(2,1)} %pad_maximum_fusion.13), channel_id=1, source_target_pairs={{0,1},{1,0},{2,3},{3,2},{4,5},{5,4},{6,7},{7,6},{8,9},{9,8},{10,11... | collective-permute-start | bytes 3538952 | tf_op jit(solution)/shard_map/ppermute | solution.py:637
  93.4 96.6 %collective-permute-start.9 = (bf16[384,384]{1,0:T(8,128)(2,1)}, bf16[384,384]{1,0:T(8,128)(2,1)}, u32[]{:S(2)}, u32[]{:S(2)}) collective-permute-start(bf16[384,384]{1,0:T(8,128)(2,1)} %pad_maximum_fusion.23), channel_id=1, source_target_pairs={{0,2},{1,3},{2,0},{3,1},{4,6},{5,7},{6,4},{7,5},{8,10},{9,11},{10,... | collective-permute-start | bytes 884744 | tf_op jit(solution)/shard_map/ppermute | solution.py:637
  112.5 80.3 %collective-permute-start.16 = (bf16[1536,384]{1,0:T(8,128)(2,1)}, bf16[1536,384]{1,0:T(8,128)(2,1)}, u32[]{:S(2)}, u32[]{:S(2)}) collective-permute-start(bf16[1536,384]{1,0:T(8,128)(2,1)} %pad_maximum_fusion.14), channel_id=1, source_target_pairs={{0,2},{1,3},{2,0},{3,1},{4,6},{5,7},{6,4},{7,5},{8,10},{9,11},{10,... | collective-permute-start | bytes 3538952 | tf_op jit(solution)/shard_map/ppermute | solution.py:637
  139.7 62.8 %collective-permute-start.14 = (bf16[768,1536]{1,0:T(8,128)(2,1)}, bf16[768,1536]{1,0:T(8,128)(2,1)}, u32[]{:S(2)}, u32[]{:S(2)}) collective-permute-start(bf16[768,1536]{1,0:T(8,128)(2,1)} %pad_maximum_fusion.4), channel_id=1, source_target_pairs={{0,4},{1,5},{2,6},{3,7},{4,0},{5,1},{6,2},{7,3},{8,12},{9,13},{10,... | collective-permute-start | bytes 7077896 | tf_op jit(solution)/shard_map/ppermute | solution.py:637
  191.1 34.8 %collective-permute-start.21 = (bf16[1024,384]{0,1:T(8,128)(2,1)}, bf16[1024,384]{0,1:T(8,128)(2,1)S(1)}, u32[]{:S(2)}, u32[]{:S(2)}) collective-permute-start(bf16[1024,384]{0,1:T(8,128)(2,1)} %bitcast.18), channel_id=1, source_target_pairs={{0,2},{1,6},{2,0},{3,4},{4,3},{5,7},{6,1},{7,5},{8,10},{9,14},{10,... | collective-permute-start | bytes 2359304 | tf_op jit(solution)/shard_map/ppermute | solution.py:637
  192.8 33.2 %collective-permute-start.20 = (bf16[1024,384]{0,1:T(8,128)(2,1)}, bf16[1024,384]{0,1:T(8,128)(2,1)S(1)}, u32[]{:S(2)}, u32[]{:S(2)}) collective-permute-start(bf16[1024,384]{0,1:T(8,128)(2,1)} %bitcast.17), channel_id=1, source_target_pairs={{0,0},{1,4},{2,2},{3,6},{4,1},{5,5},{6,3},{7,7},{8,8},{9,12},{10,1... | collective-permute-start | bytes 2359304 | tf_op jit(solution)/shard_map/ppermute | solution.py:637
  196.2 20.2 %collective-permute-start.17 = (bf16[1536,768]{1,0:T(8,128)(2,1)S(1)}, bf16[1536,768]{1,0:T(8,128)(2,1)S(1)}, u32[]{:S(2)}, u32[]{:S(2)}) collective-permute-start(bf16[1536,768]{1,0:T(8,128)(2,1)S(1)} %pad_maximum_fusion.5), channel_id=1, source_target_pairs={{0,4},{1,5},{2,6},{3,7},{4,0},{5,1},{6,2},{7,3},{8,12},{9,13},{10,... | collective-permute-start | bytes 7077896 | tf_op jit(solution)/shard_map/ppermute | solution.py:637
  283.6 20.6 %collective-permute-start.36 = (bf16[384,768]{1,0:T(8,128)(2,1)}, bf16[384,768]{1,0:T(8,128)(2,1)}, u32[]{:S(2)}, u32[]{:S(2)}) collective-permute-start(bf16[384,768]{1,0:T(8,128)(2,1)} %convolution_convert_fusion.4), channel_id=1, source_target_pairs={{0,4},{1,5},{2,6},{3,7},{4,0},{5,1},{6,2},{7,3},{8,12},{9,13},{10,... | collective-permute-start | bytes 1769480 | tf_op jit(solution)/shard_map/ppermute | solution.py:637
  289.2 17.9 %collective-permute-start.22 = (bf16[1024,384]{1,0:T(8,128)(2,1)S(1)}, bf16[1024,384]{1,0:T(8,128)(2,1)S(1)}, u32[]{:S(2)}, u32[]{:S(2)}) collective-permute-start(bf16[1024,384]{1,0:T(8,128)(2,1)S(1)} %get-tuple-element.110), channel_id=1, source_target_pairs={{0,4},{1,5},{2,6},{3,7},{4,0},{5,1},{6,2},{7,3},{8,12},{9,13},{10,... | collective-permute-start | bytes 2359304 | tf_op jit(solution)/shard_map/ppermute | solution.py:637
  295.1 109.1 %collective-permute-start.18 = (bf16[1024,384]{0,1:T(8,128)(2,1)}, bf16[1024,384]{0,1:T(8,128)(2,1)}, u32[]{:S(2)}, u32[]{:S(2)}) collective-permute-start(bf16[1024,384]{0,1:T(8,128)(2,1)} %get-tuple-element.115), channel_id=1, source_target_pairs={{0,0},{1,4},{2,2},{3,6},{4,1},{5,5},{6,3},{7,7},{8,8},{9,12},{10,1... | collective-permute-start | bytes 2359304 | tf_op jit(solution)/shard_map/ppermute | solution.py:637
  302.5 103.3 %collective-permute-start.19 = (bf16[1024,384]{0,1:T(8,128)(2,1)}, bf16[1024,384]{0,1:T(8,128)(2,1)}, u32[]{:S(2)}, u32[]{:S(2)}) collective-permute-start(bf16[1024,384]{0,1:T(8,128)(2,1)} %get-tuple-element.116), channel_id=1, source_target_pairs={{0,2},{1,6},{2,0},{3,4},{4,3},{5,7},{6,1},{7,5},{8,10},{9,14},{10,... | collective-permute-start | bytes 2359304 | tf_op jit(solution)/shard_map/ppermute | solution.py:637
  303.0 189.1 %collective-permute-start.55 = (bf16[1536,768]{1,0:T(8,128)(2,1)}, bf16[1536,768]{1,0:T(8,128)(2,1)}, u32[]{:S(2)}, u32[]{:S(2)}) collective-permute-start(bf16[1536,768]{1,0:T(8,128)(2,1)} %convolution_convert_fusion), channel_id=1, source_target_pairs={{0,4},{1,5},{2,6},{3,7},{4,0},{5,1},{6,2},{7,3},{8,12},{9,13},{10,... | collective-permute-start | bytes 7077896 | tf_op jit(solution)/shard_map/ppermute | solution.py:637
  307.0 95.4 %collective-permute-start.37 = (bf16[192,768]{1,0:T(8,128)(2,1)}, bf16[192,768]{1,0:T(8,128)(2,1)S(1)}, u32[]{:S(2)}, u32[]{:S(2)}) collective-permute-start(bf16[192,768]{1,0:T(8,128)(2,1)} %slice.321), channel_id=1, source_target_pairs={{0,1},{1,0},{2,3},{3,2},{4,5},{5,4},{6,7},{7,6},{8,9},{9,8},{10,11... | collective-permute-start | bytes 884744 | tf_op jit(solution)/shard_map/ppermute | solution.py:637
  402.5 100.4 %collective-permute-start.49 = (bf16[768,1536]{1,0:T(8,128)(2,1)}, bf16[768,1536]{1,0:T(8,128)(2,1)}, u32[]{:S(2)}, u32[]{:S(2)}) collective-permute-start(bf16[768,1536]{1,0:T(8,128)(2,1)} %convolution_convert_fusion.1), channel_id=1, source_target_pairs={{0,4},{1,5},{2,6},{3,7},{4,0},{5,1},{6,2},{7,3},{8,12},{9,13},{10,... | collective-permute-start | bytes 7077896 | tf_op jit(solution)/shard_map/ppermute | solution.py:637
  402.5 51.6 %collective-permute-start.26 = (bf16[384,3,2,192]{0,3,2,1:T(8,128)(2,1)}, bf16[384,3,2,192]{0,3,2,1:T(8,128)(2,1)}, u32[]{:S(2)}, u32[]{:S(2)}) collective-permute-start(bf16[384,3,2,192]{0,3,2,1:T(8,128)(2,1)} %bitcast.110), channel_id=1, source_target_pairs={{0,2},{1,3},{2,0},{3,1},{4,6},{5,7},{6,4},{7,5},{8,10},{9,11},{10,... | collective-permute-start | bytes 2654216 | tf_op jit(solution)/shard_map/ppermute | solution.py:637
  405.8 22.1 %collective-permute-start.38 = (bf16[192,384]{1,0:T(8,128)(2,1)S(1)}, bf16[192,384]{1,0:T(8,128)(2,1)S(1)}, u32[]{:S(2)}, u32[]{:S(2)}) collective-permute-start(bf16[192,384]{1,0:T(8,128)(2,1)S(1)} %slice.323), channel_id=1, source_target_pairs={{0,2},{1,3},{2,0},{3,1},{4,6},{5,7},{6,4},{7,5},{8,10},{9,11},{10,... | collective-permute-start | bytes 442376 | tf_op jit(solution)/shard_map/ppermute | solution.py:637
  408.8 34.1 %collective-permute-start.34 = (f32[2,192]{1,0:T(2,128)S(1)}, f32[2,192]{1,0:T(2,128)S(1)}, u32[]{:S(2)}, u32[]{:S(2)}) collective-permute-start(f32[2,192]{1,0:T(2,128)S(1)} %add.306), channel_id=1, source_target_pairs={{0,16},{1,17},{2,18},{3,19},{4,20},{5,21},{6,22},{7,23},{8,24},{9,... | collective-permute-start | bytes 4616 | tf_op jit(solution)/shard_map/ppermute | solution.py:637
  427.9 14.9 %collective-permute-start.39 = (bf16[192,384]{1,0:T(8,128)(2,1)S(1)}, bf16[192,384]{1,0:T(8,128)(2,1)S(1)}, u32[]{:S(2)}, u32[]{:S(2)}) collective-permute-start(bf16[192,384]{1,0:T(8,128)(2,1)S(1)} %add_convert_fusion.21), channel_id=1, source_target_pairs={{0,8},{1,9},{2,10},{3,11},{4,12},{5,13},{6,14},{7,15},{8,0},{9,1},... | collective-permute-start | bytes 442376 | tf_op jit(solution)/shard_map/ppermute | solution.py:637
  442.9 45.9 %collective-permute-start.61 = (bf16[3,512,512]{2,1,0:T(8,128)(2,1)}, bf16[3,512,512]{2,1,0:T(8,128)(2,1)S(1)}, u32[]{:S(2)}, u32[]{:S(2)}) collective-permute-start(bf16[3,512,512]{2,1,0:T(8,128)(2,1)} %slice.415), channel_id=1, source_target_pairs={{0,1},{1,0},{2,3},{3,2},{4,5},{5,4},{6,7},{7,6},{8,9},{9,8},{10,11... | collective-permute-start | bytes 4718600 | tf_op jit(solution)/shard_map/ppermute | solution.py:637
  456.2 31.9 %collective-permute-start.27 = (bf16[384,3,192]{0,2,1:T(8,128)(2,1)S(1)}, bf16[384,3,192]{0,2,1:T(8,128)(2,1)S(1)}, u32[]{:S(2)}, u32[]{:S(2)}) collective-permute-start(bf16[384,3,192]{0,2,1:T(8,128)(2,1)S(1)} %slice_bitcast_fusion), channel_id=1, source_target_pairs={{0,1},{1,0},{2,3},{3,2},{4,5},{5,4},{6,7},{7,6},{8,9},{9,8},{10,11... | collective-permute-start | bytes 1327112 | tf_op jit(solution)/shard_map/ppermute | solution.py:637
  458.9 40.7 %collective-permute-start.23 = (bf16[1024,768]{0,1:T(8,128)(2,1)S(1)}, bf16[1024,768]{0,1:T(8,128)(2,1)S(1)}, u32[]{:S(2)}, u32[]{:S(2)}) collective-permute-start(bf16[1024,768]{0,1:T(8,128)(2,1)S(1)} %copy-done.30), channel_id=1, source_target_pairs={{0,4},{1,5},{2,6},{3,7},{4,0},{5,1},{6,2},{7,3},{8,12},{9,13},{10,... | collective-permute-start | bytes 4718600 | tf_op jit(solution)/shard_map/ppermute | solution.py:637
  491.6 35.8 %collective-permute-start.62 = (bf16[3,4,2,32,512]{4,3,1,0,2:T(8,128)(2,1)S(1)}, bf16[3,4,2,32,512]{4,3,1,0,2:T(8,128)(2,1)S(1)}, u32[]{:S(2)}, u32[]{:S(2)}) collective-permute-start(bf16[3,4,2,32,512]{4,3,1,0,2:T(8,128)(2,1)S(1)} %bitcast.112), channel_id=1, source_target_pairs={{0,2},{1,3},{2,0},{3,1},{4,6},{5,7},{6,4},{7,5},{8,10},{9,11},{10,... | collective-permute-start | bytes 2359304 | tf_op jit(solution)/shard_map/ppermute | solution.py:637
  499.1 46.0 %collective-permute-start.56 = (bf16[768,768]{1,0:T(8,128)(2,1)}, bf16[768,768]{1,0:T(8,128)(2,1)}, u32[]{:S(2)}, u32[]{:S(2)}) collective-permute-start(bf16[768,768]{1,0:T(8,128)(2,1)} %slice.343), channel_id=1, source_target_pairs={{0,1},{1,0},{2,3},{3,2},{4,5},{5,4},{6,7},{7,6},{8,9},{9,8},{10,11... | collective-permute-start | bytes 3538952 | tf_op jit(solution)/shard_map/ppermute | solution.py:637
  501.0 28.2 %collective-permute-start.24 = (bf16[1024,384]{0,1:T(8,128)(2,1)S(1)}, bf16[1024,384]{0,1:T(8,128)(2,1)S(1)}, u32[]{:S(2)}, u32[]{:S(2)}) collective-permute-start(bf16[1024,384]{0,1:T(8,128)(2,1)S(1)} %get-tuple-element.107), channel_id=1, source_target_pairs={{0,0},{1,4},{2,2},{3,6},{4,1},{5,5},{6,3},{7,7},{8,8},{9,12},{10,1... | collective-permute-start | bytes 2359304 | tf_op jit(solution)/shard_map/ppermute | solution.py:637
  501.8 40.6 %collective-permute-start.25 = (bf16[1024,384]{0,1:T(8,128)(2,1)S(1)}, bf16[1024,384]{0,1:T(8,128)(2,1)S(1)}, u32[]{:S(2)}, u32[]{:S(2)}) collective-permute-start(bf16[1024,384]{0,1:T(8,128)(2,1)S(1)} %get-tuple-element.108), channel_id=1, source_target_pairs={{0,2},{1,6},{2,0},{3,4},{4,3},{5,7},{6,1},{7,5},{8,10},{9,14},{10,... | collective-permute-start | bytes 2359304 | tf_op jit(solution)/shard_map/ppermute | solution.py:637
  502.8 22.5 %collective-permute-start.29 = (bf16[384,3,192]{0,2,1:T(8,128)(2,1)S(1)}, bf16[384,3,192]{0,2,1:T(8,128)(2,1)S(1)}, u32[]{:S(2)}, u32[]{:S(2)}) collective-permute-start(bf16[384,3,192]{0,2,1:T(8,128)(2,1)S(1)} %add_convert_fusion.16), channel_id=1, source_target_pairs={{0,16},{1,17},{2,18},{3,19},{4,20},{5,21},{6,22},{7,23},{8,24},{9,... | collective-permute-start | bytes 1327112 | tf_op jit(solution)/shard_map/ppermute | solution.py:637
  525.3 29.2 %collective-permute-start.50 = (bf16[384,1536]{1,0:T(8,128)(2,1)}, bf16[384,1536]{1,0:T(8,128)(2,1)}, u32[]{:S(2)}, u32[]{:S(2)}) collective-permute-start(bf16[384,1536]{1,0:T(8,128)(2,1)} %slice.336), channel_id=1, source_target_pairs={{0,2},{1,3},{2,0},{3,1},{4,6},{5,7},{6,4},{7,5},{8,10},{9,11},{10,... | collective-permute-start | bytes 3538952 | tf_op jit(solution)/shard_map/ppermute | solution.py:637
  527.4 20.6 %collective-permute-start.30 = (bf16[384,3,192]{0,2,1:T(8,128)(2,1)}, bf16[384,3,192]{0,2,1:T(8,128)(2,1)}, u32[]{:S(2)}, u32[]{:S(2)}) collective-permute-start(bf16[384,3,192]{0,2,1:T(8,128)(2,1)} %add_convert_fusion.15), channel_id=1, source_target_pairs={{0,4},{1,5},{2,6},{3,7},{4,0},{5,1},{6,2},{7,3},{8,12},{9,13},{10,... | collective-permute-start | bytes 1327112 | tf_op jit(solution)/shard_map/ppermute | solution.py:637
  529.1 38.0 %collective-permute-start.63 = (bf16[3,4,32,512]{3,2,1,0:T(8,128)(2,1)S(1)}, bf16[3,4,32,512]{3,2,1,0:T(8,128)(2,1)}, u32[]{:S(2)}, u32[]{:S(2)}) collective-permute-start(bf16[3,4,32,512]{3,2,1,0:T(8,128)(2,1)S(1)} %dynamic-slice_bitcast_fusion.1), channel_id=1, source_target_pairs={{0,4},{1,5},{2,6},{3,7},{4,0},{5,1},{6,2},{7,3},{8,12},{9,13},{10,... | collective-permute-start | bytes 1179656 | tf_op jit(solution)/shard_map/ppermute | solution.py:637
  547.2 19.6 %collective-permute-start.57 = (bf16[768,384]{1,0:T(8,128)(2,1)S(1)}, bf16[768,384]{1,0:T(8,128)(2,1)S(1)}, u32[]{:S(2)}, u32[]{:S(2)}) collective-permute-start(bf16[768,384]{1,0:T(8,128)(2,1)S(1)} %slice.345), channel_id=1, source_target_pairs={{0,2},{1,3},{2,0},{3,1},{4,6},{5,7},{6,4},{7,5},{8,10},{9,11},{10,... | collective-permute-start | bytes 1769480 | tf_op jit(solution)/shard_map/ppermute | solution.py:637
  556.1 15.1 %collective-permute-start.51 = (bf16[384,768]{1,0:T(8,128)(2,1)S(1)}, bf16[384,768]{1,0:T(8,128)(2,1)S(1)}, u32[]{:S(2)}, u32[]{:S(2)}) collective-permute-start(bf16[384,768]{1,0:T(8,128)(2,1)S(1)} %slice.338), channel_id=1, source_target_pairs={{0,1},{1,0},{2,3},{3,2},{4,5},{5,4},{6,7},{7,6},{8,9},{9,8},{10,11... | collective-permute-start | bytes 1769480 | tf_op jit(solution)/shard_map/ppermute | solution.py:637
  567.0 24.7 %collective-permute-start.58 = (bf16[768,384]{1,0:T(8,128)(2,1)S(1)}, bf16[768,384]{1,0:T(8,128)(2,1)S(1)}, u32[]{:S(2)}, u32[]{:S(2)}) collective-permute-start(bf16[768,384]{1,0:T(8,128)(2,1)S(1)} %add_convert_fusion.10), channel_id=1, source_target_pairs={{0,8},{1,9},{2,10},{3,11},{4,12},{5,13},{6,14},{7,15},{8,0},{9,1},... | collective-permute-start | bytes 1769480 | tf_op jit(solution)/shard_map/ppermute | solution.py:637
  571.4 33.1 %collective-permute-start.52 = (bf16[384,768]{1,0:T(8,128)(2,1)S(1)}, bf16[384,768]{1,0:T(8,128)(2,1)}, u32[]{:S(2)}, u32[]{:S(2)}) collective-permute-start(bf16[384,768]{1,0:T(8,128)(2,1)S(1)} %add_convert_fusion.13), channel_id=1, source_target_pairs={{0,8},{1,9},{2,10},{3,11},{4,12},{5,13},{6,14},{7,15},{8,0},{9,1},... | collective-permute-start | bytes 1769480 | tf_op jit(solution)/shard_map/ppermute | solution.py:637
  572.3 34.7 %collective-permute-start.64 = (bf16[6,2,32,512]{3,2,0,1:T(8,128)(2,1)}, bf16[6,2,32,512]{3,2,0,1:T(8,128)(2,1)}, u32[]{:S(2)}, u32[]{:S(2)}) collective-permute-start(bf16[6,2,32,512]{3,2,0,1:T(8,128)(2,1)} %bitcast.93), channel_id=1, source_target_pairs={{0,16},{1,17},{2,18},{3,19},{4,20},{5,21},{6,22},{7,23},{8,24},{9,... | collective-permute-start | bytes 1179656 | tf_op jit(solution)/shard_map/ppermute | solution.py:637
  591.9 48.9 %collective-permute-start.59 = (bf16[768,384]{1,0:T(8,128)(2,1)S(1)}, bf16[768,384]{1,0:T(8,128)(2,1)}, u32[]{:S(2)}, u32[]{:S(2)}) collective-permute-start(bf16[768,384]{1,0:T(8,128)(2,1)S(1)} %add_convert_fusion.9), channel_id=1, source_target_pairs={{0,16},{1,17},{2,18},{3,19},{4,20},{5,21},{6,22},{7,23},{8,24},{9,... | collective-permute-start | bytes 1769480 | tf_op jit(solution)/shard_map/ppermute | solution.py:637
  605.7 46.7 %collective-permute-start.53 = (bf16[384,768]{1,0:T(8,128)(2,1)S(1)}, bf16[384,768]{1,0:T(8,128)(2,1)S(1)}, u32[]{:S(2)}, u32[]{:S(2)}) collective-permute-start(bf16[384,768]{1,0:T(8,128)(2,1)S(1)} %add_convert_fusion.12), channel_id=1, source_target_pairs={{0,16},{1,17},{2,18},{3,19},{4,20},{5,21},{6,22},{7,23},{8,24},{9,... | collective-permute-start | bytes 1769480 | tf_op jit(solution)/shard_map/ppermute | solution.py:637
  642.0 16.8 %collective-permute-start.60 = (bf16[768,384]{1,0:T(8,128)(2,1)S(1)}, bf16[768,384]{1,0:T(8,128)(2,1)S(1)}, u32[]{:S(2)}, u32[]{:S(2)}) collective-permute-start(bf16[768,384]{1,0:T(8,128)(2,1)S(1)} %add_convert_fusion.8), channel_id=1, source_target_pairs={{0,4},{1,5},{2,6},{3,7},{4,0},{5,1},{6,2},{7,3},{8,12},{9,13},{10,... | collective-permute-start | bytes 1769480 | tf_op jit(solution)/shard_map/ppermute | solution.py:637
  642.1 14.4 %collective-permute-start.65 = (bf16[6,1,32,512]{3,2,0,1:T(8,128)(2,1)S(1)}, bf16[6,1,32,512]{3,2,0,1:T(8,128)(2,1)S(1)}, u32[]{:S(2)}, u32[]{:S(2)}) collective-permute-start(bf16[6,1,32,512]{3,2,0,1:T(8,128)(2,1)S(1)} %constant_dynamic-slice_fusion), channel_id=1, source_target_pairs={{0,8},{1,9},{2,10},{3,11},{4,12},{5,13},{6,14},{7,15},{8,0},{9,1},... | collective-permute-start | bytes 589832 | tf_op jit(solution)/shard_map/ppermute | solution.py:637
  (82 other events, 944.8 us)
